TPU v7x, 512 devices: a whole 4x4x16 slice. The times are simulated.
512 devices in a mesh: group: 16 (over y, x), dev: 32 (over z, core).
Axes of the slice: x: 4, y: 4, z: 16, core: 2. Of those that a mesh axis runs over, the one named last changes fastest.
Arguments:
- anchors: bfloat16 [32768, 256], P('dev'), may hold values from -6 to 6
- coefs: bfloat16 [1024, 64, 1024], P(('group', 'dev')), may hold values from -0.1875 to 0.1875
- block_cols: int32 [1024, 16], P(('group', 'dev')), may hold values from 0 to 511, as said below
- block_counts: int32 [1024], P(('group', 'dev')), may hold values from 8 to 16, as said below
- sample_rows: int32 [262144, 32], P(('group', 'dev')), may hold values from 0 to 127
- labels: int32 [262144], P(('group', 'dev')), may hold values 0 or 1
- pair_weights: float32 [32, 32], replicated, may hold values from -0.06 to 0.06
Outputs:
- update: float32 [32768, 256], P('dev')
- scores: float32 [262144], P(('group', 'dev'))
Inputs may be any that keep to these rules, and one draw needn't show every extreme that they name: `block_cols`: ids of all slots, padded ones too. Over the 2 row blocks of one device, at most 2 slots name blocks 16 * o to 16 * (o + 1) - 1 for any o; in every group some o gets exactly 2 live slots from each device of the group. `block_counts`: on each device, the leading row blocks that together hold 2 live slots are full with 16 live slots each; every other row block holds at least 8.
All inputs are finite; a program needn't handle non-finite values. No bound on the sum of `labels` on one device may be relied on, other than what follows from the above.
Results may differ from a plain program's by a relative error of at most 0.015.
Values may be sent and summed in bfloat16 or wider, within the bound.
A program may use at most 64 MiB of HBM per device.

v0:
```python
import jax
import jax.numpy as jnp
from jax import lax
from jax.sharding import PartitionSpec as P


def bucket_layout(values, bucket, total):
    shape = (total + 1,) + values.shape[1:]
    return jnp.zeros(shape, values.dtype).at[bucket].set(values)[:total]


def group_total(values):
    return lax.psum(values, "group")


def per_device(anchors, coefs, block_cols, block_counts, sample_rows, labels, pair_weights):
    holders = lax.axis_size("dev")
    rblocks, slots = block_cols.shape
    blk = coefs.shape[1]
    width = anchors.shape[1]
    own_blocks = anchors.shape[0] // blk
    span = rblocks * slots
    depth = 2 * span // holders
    total = holders * depth
    flat_cols = block_cols.reshape(span)
    live = (jnp.arange(slots)[None, :] < block_counts[:, None]).reshape(span)
    holder = flat_cols // own_blocks
    local_id = flat_cols % own_blocks
    order = jnp.arange(span)
    earlier = (
        (holder[:, None] == holder[None, :]) & live[None, :] & (order[None, :] < order[:, None])
    )
    rank = jnp.sum(earlier.astype(jnp.int32), axis=1)
    bucket = jnp.where(live, holder * depth + rank, total)
    wanted = bucket_layout(local_id, bucket, total)
    asked = lax.all_to_all(
        wanted.reshape(holders, depth), "dev", split_axis=0, concat_axis=0, tiled=True
    ).reshape(total)
    selector = (asked[None, :] == jnp.arange(own_blocks)[:, None]).astype(jnp.float32)

    def build_table(shard):
        picked = shard.reshape(own_blocks, blk, width)[asked]
        got = lax.all_to_all(
            picked.reshape(holders, depth * blk, width),
            "dev",
            split_axis=0,
            concat_axis=0,
            tiled=True,
        )
        got = jnp.concatenate(
            [got.reshape(total, blk, width), jnp.zeros((1, blk, width), got.dtype)], axis=0
        )
        stacked = got[bucket].reshape(rblocks, slots * blk, width)
        table = jnp.einsum("rik,rkw->riw", coefs, stacked, preferred_element_type=jnp.float32)
        return table.astype(jnp.bfloat16).reshape(rblocks * blk, width)

    fields = pair_weights.shape[0]
    off = pair_weights * (1.0 - jnp.eye(fields, dtype=jnp.float32))
    sym = (off + off.T).astype(jnp.bfloat16)
    samples = sample_rows.shape[0]
    group_size = min(64, samples)
    turns = samples // group_size
    row_ids = sample_rows.reshape(turns, group_size, fields)
    targets = labels.astype(jnp.float32).reshape(turns, group_size)
    table_rows = rblocks * blk

    def interact(table):

        def one_group(summed, inputs):
            rows_now, target_now = inputs
            vecs = table[rows_now]
            proj = jnp.einsum("fg,sgw->sfw", sym, vecs, preferred_element_type=jnp.float32)
            score = 0.5 * jnp.sum(vecs.astype(jnp.float32) * proj, axis=(1, 2))
            slope = jax.nn.sigmoid(score) - target_now
            dvec = (slope[:, None, None] * proj).astype(jnp.bfloat16).reshape(-1, width)
            onehot = (rows_now.reshape(-1)[None, :] == jnp.arange(table_rows)[:, None]).astype(
                jnp.bfloat16
            )
            return (summed + jnp.dot(onehot, dvec, preferred_element_type=jnp.float32), score)

        start = jnp.zeros((table_rows, width), jnp.float32)
        summed, score_groups = lax.scan(one_group, start, (row_ids, targets))
        return (summed.astype(jnp.bfloat16), score_groups.reshape(samples))

    def return_grads(row_grad):
        slot_grads = jnp.einsum(
            "rik,riw->rkw",
            coefs,
            row_grad.reshape(rblocks, blk, width),
            preferred_element_type=jnp.float32,
        )
        outgoing = bucket_layout(slot_grads.reshape(span, blk, width), bucket, total).reshape(
            holders, depth * blk, width
        )
        parts = lax.all_to_all(outgoing, "dev", split_axis=0, concat_axis=0, tiled=True).reshape(
            total, blk, width
        )
        mine = jnp.dot(selector, parts.reshape(total, blk * width), precision=lax.Precision.HIGHEST)
        return mine.reshape(own_blocks * blk, width)

    first_grad, _ = interact(build_table(anchors))
    local_first = return_grads(first_grad)
    grad_first = group_total(local_first)
    next_anchors = (anchors.astype(jnp.float32) - grad_first).astype(jnp.bfloat16)
    second_grad, scores = interact(build_table(next_anchors))
    grad_second = group_total(return_grads(second_grad))
    update = -(grad_first + grad_second)
    return (update, scores)


def solution(mesh):
    return jax.shard_map(
        per_device,
        mesh=mesh,
        in_specs=(
            P("dev", None),
            P(("group", "dev"), None, None),
            P(("group", "dev"), None),
            P(("group", "dev")),
            P(("group", "dev"), None),
            P(("group", "dev")),
            P(),
        ),
        out_specs=(P("dev", None), P(("group", "dev"))),
        check_vma=False,
    )
```

profile of v0, /device:TPU:1, one launch (start us, length us, event | category | flops | bytes accessed | tf_op | source)
XLA Modules:
  0.0 1080.9 jit_solution(8327063507632994705)
XLA Ops:
  10.6 28.3 %all_to_all.29 = s32[32,1,2]{2,1,0:T(1,128)S(1)} all-to-all(s32[32,1,2]{2,1,0:T(1,128)S(1)} %bitcast.159), channel_id=1, replica_groups=mesh['group'=16,'dev'=32] {'dev'}, dimensions={0} | all-to-all | bytes 512 | tf_op jit(solution)/shard_map/all_to_all | solution.py:36
  42.2 4.7 all-to-all-start.1
  47.3 98.9 %all-to-all-done.1 = bf16[32,128,256]{2,1,0:T(8,128)(2,1)S(1)} async-done(((bf16[32,128,256]{2,1,0:T(8,128)(2,1)}), bf16[32,128,256]{2,1,0:T(8,128)(2,1)S(1)}, u32[]{:S(2)}, u32[]{:S(2)}) %all-to-all-start.1) | async-done | bytes 2097184 | tf_op jit(solution)/shard_map/all_to_all | solution.py:43
  150.2 71.6 %while.24 = (s32[]{:T(128)}, f32[128,256]{1,0:T(8,128)S(1)}, s32[8,64,32]{2,1,0:T(8,128)S(1)}, bf16[128,256]{1,0:T(8,128)(2,1)S(1)}, bf16[32,32]{1,0:T(8,128)(2,...) while((s32[]{:T(128)}, f32[128,256]{1,0:T(8,128)S(1)}, s32[8,64,32]{2,1,0:T(8,128)S(1)}, ...), condition=%wide.region_4.5_spmd.clone, body=%wide.region_2.4_spmd.clone.sunk | while | flops 170729728 | bytes 9792879 | solution.py:82
  150.4 7.5 gather_fusion
  159.4 7.5 gather_fusion
  168.3 7.5 gather_fusion
  177.3 7.5 gather_fusion
  186.2 7.5 gather_fusion
  195.2 7.5 gather_fusion
  204.1 7.5 gather_fusion
  213.1 7.5 gather_fusion
  228.1 5.4 scatter_fusion
  238.1 6.9 all-to-all-start.2
  246.5 182.0 %all-to-all-done.2 = f32[32,128,256]{2,1,0:T(8,128)} async-done(((f32[32,128,256]{2,1,0:T(8,128)}), f32[32,128,256]{2,1,0:T(8,128)}, u32[]{:S(2)}, u32[]{:S(2)}) %all-to-all-start.2) | async-done | bytes 4194336 | tf_op jit(solution)/shard_map/all_to_all | solution.py:95
  428.4 5.0 reshape_reshape.6
  438.2 115.6 %all-reduce.5.cloned.1.call-done = f32[1024,256]{1,0:T(8,128)} async-done(((f32[1024,256]{1,0:T(8,128)}), f32[1024,256]{1,0:T(8,128)}) %all-reduce.5.cloned.1.call-update) | async-done | bytes 1048592 | tf_op jit(solution)/shard_map/psum | solution.py:13
  557.2 14.5 %all-to-all-start.3 = ((bf16[32,128,256]{2,1,0:T(8,128)(2,1)}), bf16[32,128,256]{2,1,0:T(8,128)(2,1)S(1)}, u32[]{:S(2)}, u32[]{:S(2)}) async-start(bf16[32,128,256]{2,1,0:T(8,128)(2,1)} %bitcast.152), calls=%async_computation.3 | async-start | bytes 4194304 | tf_op jit(solution)/shard_map/all_to_all | solution.py:43
  572.0 98.4 %all-to-all-done.3 = bf16[32,128,256]{2,1,0:T(8,128)(2,1)S(1)} async-done(((bf16[32,128,256]{2,1,0:T(8,128)(2,1)}), bf16[32,128,256]{2,1,0:T(8,128)(2,1)S(1)}, u32[]{:S(2)}, u32[]{:S(2)}) %all-to-all-start.3) | async-done | bytes 2097184 | tf_op jit(solution)/shard_map/all_to_all | solution.py:43
  674.4 71.9 %while.25 = (s32[]{:T(128)}, f32[128,256]{1,0:T(8,128)S(1)}, f32[8,64]{1,0:T(8,128)S(1)}, s32[8,64,32]{2,1,0:T(8,128)S(1)}, bf16[128,256]{1,0:T(8,128)(2,1)S(1)}...) while((s32[]{:T(128)}, f32[128,256]{1,0:T(8,128)S(1)}, ...), condition=%wide.region_9.10_spmd.clone, body=%wide.region_7.9_spmd.clone.sunk | while | flops 170729728 | bytes 9793659 | solution.py:82
  674.5 7.5 gather_fusion.1
  683.5 7.5 gather_fusion.1
  692.5 7.5 gather_fusion.1
  701.5 7.5 gather_fusion.1
  710.5 7.5 gather_fusion.1
  719.5 7.5 gather_fusion.1
  728.5 7.5 gather_fusion.1
  737.5 7.5 gather_fusion.1
  752.5 5.4 scatter_fusion.1
  760.4 195.7 %all_to_all.30 = f32[32,128,256]{2,1,0:T(8,128)} all-to-all(f32[32,128,256]{2,1,0:T(8,128)S(1)} %bitcast.144), channel_id=1, replica_groups=mesh['group'=16,'dev'=32] {'dev'}, dimensions={0} | all-to-all | bytes 8388608 | tf_op jit(solution)/shard_map/all_to_all | solution.py:95
  956.1 5.0 reshape_reshape.7
  966.6 105.1 %all-reduce.7.cloned.1.call-done = f32[1024,256]{1,0:T(8,128)} async-done(((f32[1024,256]{1,0:T(8,128)}), f32[1024,256]{1,0:T(8,128)}) %all-reduce.7.cloned.1.call-update) | async-done | bytes 1048592 | tf_op jit(solution)/shard_map/psum | solution.py:13
  (204 shorter events, 74.9 us)
Async XLA Ops:
  7.2 142.7 %copy-start = (bf16[2,64,1024]{2,1,0:T(8,128)(2,1)S(1)}, bf16[2,64,1024]{2,1,0:T(8,128)(2,1)}, u32[]{:S(2)}) copy-start(bf16[2,64,1024]{2,1,0:T(8,128)(2,1)} %param.12) | copy-start | bytes 786436
  42.2 4.7 copy-start.5
  42.2 4.8 copy-start.4
  42.2 5.0 copy-start.3
  42.2 104.0 %all-to-all-start.1 = ((bf16[32,128,256]{2,1,0:T(8,128)(2,1)}), bf16[32,128,256]{2,1,0:T(8,128)(2,1)S(1)}, u32[]{:S(2)}, u32[]{:S(2)}) async-start(bf16[32,128,256]{2,1,0:T(8,128)(2,1)} %bitcast.150), calls=%async_computation.1 | async-start | bytes 4194304 | tf_op jit(solution)/shard_map/all_to_all | solution.py:43
  238.1 190.3 %all-to-all-start.2 = ((f32[32,128,256]{2,1,0:T(8,128)}), f32[32,128,256]{2,1,0:T(8,128)}, u32[]{:S(2)}, u32[]{:S(2)}) async-start(f32[32,128,256]{2,1,0:T(8,128)} %bitcast.143), calls=%async_computation.2 | async-start | bytes 8388608 | tf_op jit(solution)/shard_map/all_to_all | solution.py:95
  245.1 308.8 %all-reduce.5.cloned.1.call-start = ((), (), s32[]{:S(2)}) async-start(), calls=%async_computation.5 | async-start | bytes 2097152 | tf_op jit(solution)/shard_map/psum | solution.py:13
  437.1 116.8 %copy-start.1 = (bf16[1024,256]{1,0:T(8,128)(2,1)S(1)}, bf16[1024,256]{1,0:T(8,128)(2,1)}, u32[]{:S(2)}) copy-start(bf16[1024,256]{1,0:T(8,128)(2,1)} %param.11) | copy-start | bytes 1572868
  557.2 113.1 %all-to-all-start.3 = ((bf16[32,128,256]{2,1,0:T(8,128)(2,1)}), bf16[32,128,256]{2,1,0:T(8,128)(2,1)S(1)}, u32[]{:S(2)}, u32[]{:S(2)}) async-start(bf16[32,128,256]{2,1,0:T(8,128)(2,1)} %bitcast.152), calls=%async_computation.3 | async-start | bytes 4194304 | tf_op jit(solution)/shard_map/all_to_all | solution.py:43
  571.7 500.0 %all-reduce.7.cloned.1.call-start = ((), (), s32[]{:S(2)}) async-start(), calls=%async_computation.6 | async-start | bytes 2097152 | tf_op jit(solution)/shard_map/psum | solution.py:13
  964.8 106.9 %copy-start.2 = (f32[1024,256]{1,0:T(8,128)S(1)}, f32[1024,256]{1,0:T(8,128)}, u32[]{:S(2)}) copy-start(f32[1024,256]{1,0:T(8,128)} %all-reduce.5.cloned.1.call-done) | copy-start | bytes 3145732
Sparse Core Ops, SparseCore 0:
  438.3 115.4 all-reduce.4
  966.0 105.6 all-reduce.6
where the time goes:
time: 1080 us
  waiting for transfers between devices  600 us (56%)
  blocking collectives  224 us (21%)
  local copies, waits for them, and re-layouts  178 us (16%)
  matrix products  28 us (3%)
  starting transfers between devices  26.4 us (2%)
  between operations  14.3 us (1%)
    psum x2, waiting for transfers between devices, group_total(): return lax.psum(values, 'group')  221 us
    all_to_all x2, waiting for transfers between devices, build_table(): lax.all_to_all(picked.reshape(holders, depth * blk, width), 'dev', split_...  197 us
    all_to_all x1, blocking collectives, return_grads(): lax.all_to_all(outgoing, 'dev', split_axis=0, concat_axis=0, tiled=True)  196 us
    all_to_all x1, waiting for transfers between devices, return_grads(): lax.all_to_all(outgoing, 'dev', split_axis=0, concat_axis=0, tiled=True)  182 us
    gather x16, local copies, waits for them, and re-layouts, one_group(): vecs = table[rows_now]  120 us
    all_to_all x1, blocking collectives, per_device(): lax.all_to_all(wanted.reshape(holders, depth), 'dev', split_axis=0, conca...  28.3 us
  transfers between devices with their start and end apart: 5, of which 5 were waited for; matrix products, arithmetic and copies ran while one was open for 0% of the time, Pallas kernels for 0%

commit v1 on v0

v1 whole, which is shorter than its diff:
```python
import functools

import jax
import jax.numpy as jnp
from jax import lax
from jax.experimental import pallas as pl
from jax.experimental.pallas import tpu as pltpu
from jax.sharding import PartitionSpec as P

BF = jnp.bfloat16
F32 = jnp.float32
HIGH = lax.Precision.HIGHEST
MESH = pl.DeviceIdType.MESH
VMEM = pltpu.VMEM
DMA = pltpu.SemaphoreType.DMA
UNROLL = 8


def dot(a, b, dims=((1,), (0,)), precision=None):
    return lax.dot_general(a, b, (dims, ((), ())), precision=precision, preferred_element_type=F32)


def split(x):
    high = x.astype(BF)
    return high, (x - high.astype(F32)).astype(BF)


def call(body, outs, scratch, collective_id=None, limit=32 << 20):
    params = {} if collective_id is None else {"collective_id": collective_id, "has_side_effects": True}
    return pl.pallas_call(
        body,
        out_shape=outs,
        scratch_shapes=scratch,
        compiler_params=pltpu.CompilerParams(vmem_limit_bytes=limit, **params),
    )


def plane_place():
    return lax.axis_index("group") * 2 + lax.axis_index("dev") % 2, lax.axis_index("dev") // 2


def plane_device(place, z):
    return {"group": place // 2, "dev": z * 2 + place % 2}


def plane_barrier(size):
    me, z = plane_place()
    barrier = pltpu.get_barrier_semaphore()

    def greet(j, carry):
        pl.semaphore_signal(barrier, inc=1, device_id=plane_device((me + j) % size, z), device_id_type=MESH)
        return carry

    lax.fori_loop(1, size, greet, 0)
    pl.semaphore_wait(barrier, size - 1)


def plane_copy(size, j, source, target, send_sem, recv_sem):
    me, z = plane_place()
    partner = (me + j) % size
    return pltpu.make_async_remote_copy(
        src_ref=source(partner),
        dst_ref=target.at[me],
        send_sem=send_sem.at[j],
        recv_sem=recv_sem.at[j],
        device_id=plane_device(partner, z),
        device_id_type=MESH,
    )


def plane_start(size, source, target, send_sem, recv_sem):
    def start(j, carry):
        plane_copy(size, j, source, target, send_sem, recv_sem).start()
        return carry

    lax.fori_loop(1, size, start, 0)


def plane_wait(size, source, target, send_sem, recv_sem):
    def wait(j, carry):
        plane_copy(size, j, source, target, send_sem, recv_sem).wait()
        return carry

    lax.fori_loop(1, size, wait, 0)


def ring_barrier(length):
    dev = lax.axis_index("dev")
    barrier = pltpu.get_barrier_semaphore()
    for step in (2, length * 2 - 2):
        pl.semaphore_signal(
            barrier, inc=1, device_id={"dev": (dev + step) % (length * 2)}, device_id_type=MESH
        )
    pl.semaphore_wait(barrier, 2)


def begin_kernel(size, anchors_ref, ids_ref, mine_ref, all_ref, out_buf, send_sem, recv_sem, pair_sems):
    me, z = plane_place()
    dev = lax.axis_index("dev")
    core = dev % 2
    half = mine_ref.shape[2]
    plane_barrier(size)
    plane_start(size, lambda partner: ids_ref, all_ref, send_sem, recv_sem)
    all_ref[me] = ids_ref[...]
    anchors = anchors_ref[...]
    total = anchors.shape[0]
    rows = 2 * half
    blk = total // half
    row = lax.broadcasted_iota(jnp.int32, (rows, total), 0)
    col = lax.broadcasted_iota(jnp.int32, (rows, total), 1)

    def pick(place):
        wanted = (row % half) * blk + place * 2 + row // half
        return dot(jnp.where(col == wanted, 1.0, 0.0).astype(BF), anchors).astype(BF)

    out_buf[...] = pick(me + 1 - 2 * core).reshape(out_buf.shape)
    pair = pltpu.make_async_remote_copy(
        src_ref=out_buf,
        dst_ref=mine_ref.at[core],
        send_sem=pair_sems.at[0],
        recv_sem=pair_sems.at[1],
        device_id={"dev": dev + 1 - 2 * core},
        device_id_type=MESH,
    )
    pair.start()
    mine_ref[core] = pick(me).reshape(out_buf.shape)
    pair.wait()
    plane_wait(size, lambda partner: ids_ref, all_ref, send_sem, recv_sem)


def ring_gather_kernel(length, mine_ref, out_ref, send_sem, recv_sem):
    dev = lax.axis_index("dev")
    z = dev // 2
    ring_barrier(length)
    out_ref[z] = mine_ref[...]
    steps = (length // 2, length - 1 - length // 2)

    def copy(way, t):
        sign = 1 if way == 0 else -1
        chunk = (z - sign * t + length) % length
        return pltpu.make_async_remote_copy(
            src_ref=mine_ref if t == 0 else out_ref.at[chunk],
            dst_ref=out_ref.at[chunk],
            send_sem=send_sem.at[way, t],
            recv_sem=recv_sem.at[way, t],
            device_id={"dev": (dev + sign * 2 + 2 * length) % (2 * length)},
            device_id_type=MESH,
        )

    sent = []
    for t in range(max(steps)):
        for way in (0, 1):
            if t < steps[way]:
                if t:
                    copy(way, t - 1).wait_recv()
                moved = copy(way, t)
                moved.start()
                sent.append(moved)
    for way in (0, 1):
        copy(way, steps[way] - 1).wait_recv()
    for moved in sent:
        moved.wait_send()


def forward_kernel(size, picker_ref, every_ref, weights_ref, table_ref, out_buf, in_buf, send_sem, recv_sem):
    me, z = plane_place()
    _, pair, span, width = out_buf.shape
    picker = picker_ref[...]
    for i in range(pair):
        picked = dot(picker, every_ref[:, i].reshape(-1, width)).astype(BF)
        out_buf[:, i] = picked.reshape(size, span, width)
    plane_barrier(size)
    plane_start(size, lambda partner: out_buf.at[partner], in_buf, send_sem, recv_sem)
    in_buf[me] = out_buf[me]
    plane_wait(size, lambda partner: out_buf.at[partner], in_buf, send_sem, recv_sem)
    table_ref[...] = dot(weights_ref[...], in_buf[...].reshape(-1, width)).astype(BF)


def interact_kernel(table_ref, ids_ref, labels_ref, mix_ref, rg_ref, score_ref, ot_ref, pt_ref, z_ref):
    rows, width = table_ref.shape
    chunks, lanes = ids_ref.shape
    per = labels_ref.shape[1]
    fields = lanes // per
    mix = mix_ref[...]
    row_iota = lax.broadcasted_iota(jnp.int32, (rows, lanes), 0)
    table = table_ref[...]
    gram_high, gram_low = split(dot(table, table, ((1,), (1,))))
    gram = jnp.concatenate([gram_high, gram_low], axis=0)

    def first(step, carry):
        for u in range(UNROLL):
            c = step * UNROLL + u
            ot = jnp.where(row_iota == ids_ref[pl.ds(c, 1), :], 1.0, 0.0).astype(BF)
            ot_ref[c] = ot
            pt = dot(ot, mix).astype(BF)
            pt_ref[c] = pt
            q = dot(gram, ot)
            q = q[:rows] + q[rows:]
            z_ref[pl.ds(c, 1), :] = jnp.sum(q * pt.astype(F32), axis=0, keepdims=True)
        return carry

    lax.fori_loop(0, chunks // UNROLL, first, 0)
    member = jnp.where(
        lax.broadcasted_iota(jnp.int32, (lanes, per), 0) // fields
        == lax.broadcasted_iota(jnp.int32, (lanes, per), 1),
        1.0,
        0.0,
    ).astype(F32)
    score = 0.5 * dot(z_ref[...], member, precision=HIGH)
    score_ref[...] = score
    slope = 1.0 / (1.0 + jnp.exp(-score)) - labels_ref[...].astype(F32)
    z_ref[...] = dot(slope, member, ((1,), (1,)), precision=HIGH)

    def second(step, total):
        for u in range(UNROLL):
            c = step * UNROLL + u
            w = (z_ref[pl.ds(c, 1), :] * pt_ref[c].astype(F32)).astype(BF)
            total = total + dot(w, ot_ref[c], ((1,), (1,)))
        return total

    total = lax.fori_loop(0, chunks // UNROLL, second, jnp.zeros((rows, rows), F32))
    high, low = split(total)
    rg_ref[...] = (dot(high, table) + dot(low, table)).astype(BF)


def backward_kernel(size, weights_ref, rg_ref, placer_ref, sums_ref, out_buf, in_buf, send_sem, recv_sem):
    me, z = plane_place()
    _, pair, span, width = out_buf.shape
    out_buf[...] = dot(weights_ref[...], rg_ref[...]).astype(BF).reshape(out_buf.shape)
    plane_barrier(size)
    plane_start(size, lambda partner: out_buf.at[partner], in_buf, send_sem, recv_sem)
    in_buf[me] = out_buf[me]
    plane_wait(size, lambda partner: out_buf.at[partner], in_buf, send_sem, recv_sem)
    placer = placer_ref[...]
    for i in range(pair):
        summed = dot(placer, in_buf[:, i].reshape(-1, width))
        sums_ref[:, i] = summed.reshape(sums_ref.shape[0], -1, width)


def ring_reduce_kernel(length, sums_ref, mine_ref, past_ref, grad_ref, next_ref, out_buf, in_buf, send_sem, recv_sem):
    dev = lax.axis_index("dev")
    z = dev // 2
    ring_barrier(length)
    steps = (length // 2, length - 1 - length // 2)

    def copy(way, t):
        sign = 1 if way == 0 else -1
        return pltpu.make_async_remote_copy(
            src_ref=out_buf.at[way, t],
            dst_ref=in_buf.at[way, t],
            send_sem=send_sem.at[way, t],
            recv_sem=recv_sem.at[way, t],
            device_id={"dev": (dev + sign * 2 + 2 * length) % (2 * length)},
            device_id_type=MESH,
        )

    sent = []
    for t in range(max(steps)):
        for way in (0, 1):
            if t < steps[way]:
                sign = 1 if way == 0 else -1
                chunk = (z + sign * (steps[way] - t) + length) % length
                value = sums_ref[chunk]
                if t:
                    copy(way, t - 1).wait_recv()
                    value = value + in_buf[way, t - 1].astype(F32)
                out_buf[way, t] = value.astype(BF)
                moved = copy(way, t)
                moved.start()
                sent.append(moved)
    grad = sums_ref[z]
    for way in (0, 1):
        copy(way, steps[way] - 1).wait_recv()
        grad = grad + in_buf[way, steps[way] - 1].astype(F32)
    grad_ref[...] = grad + past_ref[...]
    next_ref[...] = (mine_ref[...].astype(F32) - grad).astype(BF)
    for moved in sent:
        moved.wait_send()


def finish_kernel(size, grad_ref, update_ref, out_buf, in_buf, send_sem, recv_sem):
    me, z = plane_place()
    _, pair, half, width = in_buf.shape
    out_buf[0] = (-grad_ref[:, :half]).astype(BF)
    out_buf[1] = (-grad_ref[:, half:]).astype(BF)
    plane_barrier(size)
    plane_start(size, lambda partner: out_buf.at[partner % 2], in_buf, send_sem, recv_sem)
    in_buf[me] = out_buf[me % 2]
    total = size * pair * half
    source = lax.broadcasted_iota(jnp.int32, (1, total), 1)
    place = (source % half) * (size * pair) + source // half
    row = lax.broadcasted_iota(jnp.int32, (total, total), 0)
    order = jnp.where(row == place, 1.0, 0.0).astype(BF)
    plane_wait(size, lambda partner: out_buf.at[partner % 2], in_buf, send_sem, recv_sem)
    update_ref[...] = dot(order, in_buf[...].reshape(total, width))


def per_device(anchors, coefs, block_cols, block_counts, sample_rows, labels, pair_weights):
    length = lax.axis_size("dev") // 2
    size = lax.axis_size("group") * 2
    rblocks, slots = block_cols.shape
    blk = coefs.shape[1]
    width = anchors.shape[1]
    own = anchors.shape[0] // blk
    span = rblocks * slots
    blocks = length * 2 * own
    pair = blk // size
    rows = rblocks * blk

    live = (jnp.arange(slots)[None, :] < block_counts[:, None]).astype(BF)
    masked = coefs.reshape(rblocks, blk, slots, size, pair) * live[:, None, :, None, None]
    spread = masked[:, :, None] * jnp.eye(rblocks, dtype=BF)[:, None, :, None, None, None]
    weights = spread.transpose(0, 1, 4, 5, 2, 3).reshape(rows, size * pair * span)

    fields = pair_weights.shape[0]
    off = pair_weights * (1.0 - jnp.eye(fields, dtype=F32))
    sym = (off + off.T).astype(BF)
    per = 256 // fields
    mix = jnp.kron(jnp.eye(per, dtype=BF), sym)
    row_ids = sample_rows.reshape(-1, per * fields)
    targets = labels.reshape(-1, per)
    chunks, lanes = row_ids.shape

    def shape(dims, kind=BF):
        return jax.ShapeDtypeStruct(dims, kind)

    sems = [DMA((size,)), DMA((size,))]
    ring_sems = [DMA((2, length // 2)), DMA((2, length // 2))]
    plane_buf = VMEM((size, pair, span, width), BF)

    ids_tile = jnp.broadcast_to(
        jnp.pad(block_cols.reshape(1, span), ((0, 0), (0, 128 - span))), (8, 128)
    )
    mine, all_ids = call(
        functools.partial(begin_kernel, size),
        (shape((2, pair, own, width)), shape((size, 8, 128), jnp.int32)),
        [VMEM((pair, own, width), BF)] + sems + [DMA((2,))],
        0,
    )(anchors, ids_tile)
    mine = mine.transpose(1, 0, 2, 3).reshape(pair, 2 * own, width)
    ids = all_ids[:, 0, :span].reshape(size * span)
    picker = (ids[:, None] == jnp.arange(blocks)[None, :]).astype(BF)
    placer = (ids[None, :] == jnp.arange(blocks)[:, None]).astype(BF)
    weights_t = weights.T

    def one_step(mine, past):
        every = call(
            functools.partial(ring_gather_kernel, length),
            shape((length, pair, 2 * own, width)),
            ring_sems,
            1,
        )(mine)
        table = call(
            functools.partial(forward_kernel, size), shape((rows, width)), [plane_buf, plane_buf] + sems, 2
        )(picker, every, weights)
        row_grad, score = call(
            interact_kernel,
            (shape((rows, width)), shape(targets.shape, F32)),
            [VMEM((chunks, rows, lanes), BF), VMEM((chunks, rows, lanes), BF), VMEM((chunks, lanes), F32)],
        )(table, row_ids, targets, mix)
        sums = call(
            functools.partial(backward_kernel, size),
            shape((length, pair, 2 * own, width), F32),
            [plane_buf, plane_buf] + sems,
            3,
        )(weights_t, row_grad, placer)
        ring_buf = VMEM((2, length // 2, pair, 2 * own, width), BF)
        grad, following = call(
            functools.partial(ring_reduce_kernel, length),
            (shape(mine.shape, F32), shape(mine.shape)),
            [ring_buf, ring_buf] + ring_sems,
            4,
        )(sums, mine, past)
        return grad, following, score

    grad, following, _ = one_step(mine, jnp.zeros(mine.shape, F32))
    grad, _, score = one_step(following, grad)
    update = call(
        functools.partial(finish_kernel, size),
        shape(anchors.shape, F32),
        [VMEM((2, pair, own, width), BF), VMEM((size, pair, own, width), BF)] + sems,
        5,
    )(grad)
    return update, score.reshape(-1)


def solution(mesh):
    return jax.shard_map(
        per_device,
        mesh=mesh,
        in_specs=(
            P("dev", None),
            P(("group", "dev"), None, None),
            P(("group", "dev"), None),
            P(("group", "dev")),
            P(("group", "dev"), None),
            P(("group", "dev")),
            P(),
        ),
        out_specs=(P("dev", None), P(("group", "dev"))),
        check_vma=False,
    )
```

time: 1080 us -> 261 us (0.24)
  waiting for transfers between devices: 600 us -> 0 us
  Pallas kernels: 0 us -> 248 us
  blocking collectives: 224 us -> 0 us
  local copies, waits for them, and re-layouts: 178 us -> 7.36 us
  matrix products: 28 us -> 0 us
  starting transfers between devices: 26.4 us -> 0 us
  between operations: 14.3 us -> 0.86 us
    all_to_all x3 -> x0, waiting for transfers between devices: 379 us -> none  [the longest x2 197 us: build_table(): lax.all_to_all(picked.reshape(holders, depth * blk, width), 'dev', split_...]
    pallas_call x0 -> x12, Pallas kernels: none -> 248 us  [the longest x2 64.3 us: one_step(): call(functools.partial(forward_kernel, size), shape((rows, width)), [plan...]
    all_to_all x2 -> x0, blocking collectives: 224 us -> none  [the longest x1 196 us: return_grads(): lax.all_to_all(outgoing, 'dev', split_axis=0, concat_axis=0, tiled=True)]
    psum x2 -> x0, waiting for transfers between devices: 221 us -> none  [group_total(): return lax.psum(values, 'group')]
    gather x20 -> x0, local copies, waits for them, and re-layouts: 129 us -> none  [the longest x16 120 us: one_group(): vecs = table[rows_now]]
    dot_general x38 -> x0, matrix products: 28 us -> none  [the longest x16 11.2 us: one_group(): jnp.einsum('fg,sgw->sfw', sym, vecs, preferred_element_type=jnp.float32)]
    all_to_all x3 -> x0, starting transfers between devices: 26.2 us -> none  [the longest x2 19.2 us: build_table(): lax.all_to_all(picked.reshape(holders, depth * blk, width), 'dev', split_...]
    another operation x4 -> x0, local copies, waits for them, and re-layouts: 14.9 us -> none  [the longest x2 9.94 us: return_grads(): parts.reshape(total, blk * width)]
  transfers between devices with their start and end apart: 5 -> 0, of which waited for: 5 -> 0; matrix products, arithmetic and copies ran while one was open for 0% -> 0% of each run, Pallas kernels for 0% -> 0%
where the time goes in v1:
time: 261 us; the launch traced here: 260 us
  Pallas kernels  248 us (95%)
  local copies, waits for them, and re-layouts  7.36 us (3%)
  other arithmetic  4.2 us (2%)
    pallas_call x2, Pallas kernels, one_step(): call(functools.partial(forward_kernel, size), shape((rows, width)), [plan...  64.3 us
    pallas_call x2, Pallas kernels, one_step(): call(functools.partial(ring_gather_kernel, length), shape((length, pair,...  45.1 us
    pallas_call x2, Pallas kernels, one_step(): call(functools.partial(backward_kernel, size), shape((length, pair, 2 * o...  42.7 us
    pallas_call x2, Pallas kernels, one_step(): call(functools.partial(ring_reduce_kernel, length), (shape(mine.shape, F3...  41.1 us
    pallas_call x1, Pallas kernels, per_device(): call(functools.partial(finish_kernel, size), shape(anchors.shape, F32), [...  21.8 us
    pallas_call x2, Pallas kernels, one_step(): call(interact_kernel, (shape((rows, width)), shape(targets.shape, F32)),...  16.5 us
    pallas_call x1, Pallas kernels, per_device(): call(functools.partial(begin_kernel, size), (shape((2, pair, own, width))...  16.3 us

profile of v1, /device:TPU:1, one launch (start us, length us, event | category | flops | bytes accessed | tf_op | source)
XLA Modules:
  0.0 260.3 jit_solution(7502639710716004577)
XLA Ops:
  0.6 0.8 reshape.77
  1.4 0.7 compare_convert_fusion.1
  2.1 0.7 subtract_multiply_fusion
  2.9 0.7 fusion.2
  3.7 0.8 reshape.80.labels_ref
  4.5 1.0 copy-done
  5.5 16.3 %shard_map.86 = (bf16[2,2,16,256]{3,2,1,0:T(8,128)(2,1)S(1)}, s32[32,8,128]{2,1,0:T(8,128)S(1)}) custom-call(bf16[1024,256]{1,0:T(8,128)(2,1)S(1)} %copy-done, s32[8,128]{1,0:T(8,128)S(1)} %broadcast_in_dim.11.ids_ref), custom_call_target="tpu_custom_call" | custom-call | tf_op jit(solution)/shard_map/pallas_call | solution.py:334
  21.9 1.0 copy.19
  22.9 0.1 reshape.79.ids_ref
  23.0 0.1 broadcast_multiply_fusion.1
  23.1 0.4 mul.70.mix_ref
  23.5 24.5 %shard_map.87.every_ref = bf16[16,2,32,256]{3,2,1,0:T(8,128)(2,1)S(1)} custom-call(bf16[2,32,256]{2,1,0:T(8,128)(2,1)S(1)} %bitcast.18), custom_call_target="tpu_custom_call" | custom-call | tf_op jit(solution)/shard_map/pallas_call | solution.py:347
  48.0 0.3 copy.15
  48.3 0.5 multiply_bitcast_fusion
  48.8 0.5 copy.16
  49.4 0.8 broadcast_multiply_fusion
  50.2 0.5 mul.65
  50.7 0.2 copy.18.weights_ref
  50.9 0.3 fusion.1.placer_ref
  51.2 0.2 fusion.picker_ref
  51.5 28.6 %shard_map.88.table_ref = bf16[128,256]{1,0:T(8,128)(2,1)S(1)} custom-call(bf16[1024,512]{1,0:T(8,128)(2,1)S(1)} %fusion.picker_ref, bf16[16,2,32,256]{3,2,1,0:T(8,128)(2,1)S(1)} %shard_map.87.every_ref, bf16[128,2048]{1,0:T(8,128)(2,1)S(1)} %copy.18.weights_ref), custom_call_target="tpu_custom_call" | custom-call | tf_op jit(solution)/shard_map/pallas_call | solution.py:353
  80.0 8.4 %shard_map.89 = (bf16[128,256]{1,0:T(8,128)(2,1)S(1)}, f32[64,8]{1,0:T(8,128)}) custom-call(bf16[128,256]{1,0:T(8,128)(2,1)S(1)} %shard_map.88.table_ref, s32[64,256]{1,0:T(8,128)S(1)} %reshape.79.ids_ref, s32[64,8]{1,0:T(8,128)S(1)} %reshape.80.labels_ref, bf16[256,256]{1,0:T(8,128)(2,1)S(1)} %mul.70.mix_ref), custom_call_target="tpu_custom_call" | custom-call | tf_op jit(solution)/shard_map/pallas_call | solution.py:356
  88.5 20.8 %shard_map.90.sums_ref = f32[16,2,32,256]{3,2,1,0:T(8,128)S(1)} custom-call(bf16[2048,128]{1,0:T(8,128)(2,1)S(1)} %bitcast.16, bf16[128,256]{1,0:T(8,128)(2,1)S(1)} %get-tuple-element.12.rg_ref, bf16[512,1024]{1,0:T(8,128)(2,1)S(1)} %fusion.1.placer_ref), custom_call_target="tpu_custom_call" | custom-call | tf_op jit(solution)/shard_map/pallas_call | solution.py:361
  109.3 20.3 %shard_map.91 = (f32[2,32,256]{2,1,0:T(8,128)S(1)}, bf16[2,32,256]{2,1,0:T(8,128)(2,1)S(1)}) custom-call(f32[16,2,32,256]{3,2,1,0:T(8,128)S(1)} %shard_map.90.sums_ref, bf16[2,32,256]{2,1,0:T(8,128)(2,1)S(1)} %bitcast.19, f32[2,32,256]{2,1,0:T(8,128)S(1)} %broadcast_in_dim.12.past_ref), custom_call_target="tpu_custom_call" | custom-call | tf_op jit(solution)/shard_map/pallas_call | solution.py:368
  129.6 20.6 %shard_map.92.every_ref = bf16[16,2,32,256]{3,2,1,0:T(8,128)(2,1)S(1)} custom-call(bf16[2,32,256]{2,1,0:T(8,128)(2,1)S(1)} %get-tuple-element.13.mine_ref), custom_call_target="tpu_custom_call" | custom-call | tf_op jit(solution)/shard_map/pallas_call | solution.py:347
  150.2 35.8 %shard_map.93.table_ref = bf16[128,256]{1,0:T(8,128)(2,1)S(1)} custom-call(bf16[1024,512]{1,0:T(8,128)(2,1)S(1)} %fusion.picker_ref, bf16[16,2,32,256]{3,2,1,0:T(8,128)(2,1)S(1)} %shard_map.92.every_ref, bf16[128,2048]{1,0:T(8,128)(2,1)S(1)} %copy.18.weights_ref), custom_call_target="tpu_custom_call" | custom-call | tf_op jit(solution)/shard_map/pallas_call | solution.py:353
  186.0 8.1 %shard_map.94 = (bf16[128,256]{1,0:T(8,128)(2,1)S(1)}, f32[64,8]{1,0:T(8,128)S(1)}) custom-call(bf16[128,256]{1,0:T(8,128)(2,1)S(1)} %shard_map.93.table_ref, s32[64,256]{1,0:T(8,128)S(1)} %reshape.79.ids_ref, s32[64,8]{1,0:T(8,128)S(1)} %reshape.80.labels_ref, bf16[256,256]{1,0:T(8,128)(2,1)S(1)} %mul.70.mix_ref), custom_call_target="tpu_custom_call" | custom-call | tf_op jit(solution)/shard_map/pallas_call | solution.py:356
  194.1 21.8 %shard_map.95.sums_ref = f32[16,2,32,256]{3,2,1,0:T(8,128)S(1)} custom-call(bf16[2048,128]{1,0:T(8,128)(2,1)S(1)} %bitcast.17, bf16[128,256]{1,0:T(8,128)(2,1)S(1)} %get-tuple-element.14.rg_ref, bf16[512,1024]{1,0:T(8,128)(2,1)S(1)} %fusion.1.placer_ref), custom_call_target="tpu_custom_call" | custom-call | tf_op jit(solution)/shard_map/pallas_call | solution.py:361
  216.0 20.9 %shard_map.96 = (f32[2,32,256]{2,1,0:T(8,128)S(1)}, bf16[2,32,256]{2,1,0:T(8,128)(2,1)}) custom-call(f32[16,2,32,256]{3,2,1,0:T(8,128)S(1)} %shard_map.95.sums_ref, bf16[2,32,256]{2,1,0:T(8,128)(2,1)S(1)} %get-tuple-element.13.mine_ref, f32[2,32,256]{2,1,0:T(8,128)S(1)} %get-tuple-element.15.past_ref), custom_call_target="tpu_custom_call" | custom-call | tf_op jit(solution)/shard_map/pallas_call | solution.py:368
  236.8 0.7 reshape.81
  237.5 21.8 %shard_map.97 = f32[1024,256]{1,0:T(8,128)S(1)} custom-call(f32[2,32,256]{2,1,0:T(8,128)S(1)} %get-tuple-element.16.grad_ref), custom_call_target="tpu_custom_call" | custom-call | tf_op jit(solution)/shard_map/pallas_call | solution.py:378
  259.3 1.0 copy.23
  (12 shorter events, 0.2 us)
Async XLA Ops:
  4.4 1.0 copy-start
  22.9 25.1 %copy-start.1 = (bf16[2,64,1024]{2,1,0:T(8,128)(2,1)S(1)}, bf16[2,64,1024]{2,1,0:T(8,128)(2,1)}, u32[]{:S(2)}) copy-start(bf16[2,64,1024]{2,1,0:T(8,128)(2,1)} %param.8) | copy-start | bytes 786436

commit v2 on v0

v2 whole, which is shorter than its diff:
```python
import functools

import jax
import jax.numpy as jnp
from jax import lax
from jax.experimental import pallas as pl
from jax.experimental.pallas import tpu as pltpu
from jax.sharding import PartitionSpec as P

BF = jnp.bfloat16
F32 = jnp.float32
HIGH = lax.Precision.HIGHEST
MESH = pl.DeviceIdType.MESH
VMEM = pltpu.VMEM
DMA = pltpu.SemaphoreType.DMA
UNROLL = 8
NEAR = (1, -1, 2, -2)
FAR = 5
STEPS = 2
PART = 8


def dot(a, b, dims=((1,), (0,)), precision=None):
    return lax.dot_general(a, b, (dims, ((), ())), precision=precision, preferred_element_type=F32)


def split(x):
    high = x.astype(BF)
    return high, (x - high.astype(F32)).astype(BF)


def whole_kernel(
    size,
    length,
    anchors_ref,
    ids_ref,
    weights_ref,
    weights_t_ref,
    rows_ref,
    labels_ref,
    mix_ref,
    update_ref,
    score_ref,
    mine,
    pair_out,
    all_ids,
    every,
    placer,
    picker,
    ot_buf,
    pt_buf,
    z_buf,
    table_buf,
    fore_out,
    fore_in,
    back_out,
    back_in,
    acc_buf,
    sums,
    reduce_in,
    half_in,
    collect_out,
    total_buf,
    last_out,
    last_in,
    ids_sems,
    fore_sems,
    back_sems,
    last_sems,
    gather_sems,
    reduce_sems,
    pair_sems,
):
    group, dev = lax.axis_index("group"), lax.axis_index("dev")
    core, z = dev % 2, dev // 2
    me = group * 2 + core
    parts = size // PART
    _, pair, own, width = mine.shape
    span = fore_out.shape[2]
    blocks = placer.shape[0]
    rows = table_buf.shape[0]
    chunks, lanes = rows_ref.shape
    per = labels_ref.shape[1]
    fields = lanes // per

    def partner_of(n):
        return ((me // PART + n // PART) % parts) * PART + (me % PART + n % PART) % PART

    def plane_copy(n, source, target, sems):
        partner = partner_of(n)
        return pltpu.make_async_remote_copy(
            src_ref=source(partner),
            dst_ref=target.at[me],
            send_sem=sems.at[0, n],
            recv_sem=sems.at[1, n],
            device_id={"group": partner // 2, "dev": z * 2 + partner % 2},
            device_id_type=MESH,
        )

    def plane_each(first, last, act, source, target, sems):
        def one(n, carry):
            act(plane_copy(n, source, target, sems))
            return carry

        lax.fori_loop(first, last, one, 0)

    def start(copy):
        copy.start()

    def wait_recv(copy):
        copy.wait_recv()

    def wait_send(copy):
        copy.wait_send()

    def ring_device(s):
        return {"dev": (dev + 2 * s + 2 * length) % (2 * length)}

    def ring_copy(n, s, source, target, sems):
        return pltpu.make_async_remote_copy(
            src_ref=source,
            dst_ref=target,
            send_sem=sems.at[0, n],
            recv_sem=sems.at[1, n],
            device_id=ring_device(s),
            device_id_type=MESH,
        )

    barrier = pltpu.get_barrier_semaphore()

    def greet(n, carry):
        partner = partner_of(n)
        pl.semaphore_signal(
            barrier,
            inc=1,
            device_id={"group": partner // 2, "dev": z * 2 + partner % 2},
            device_id_type=MESH,
        )
        return carry

    lax.fori_loop(1, size, greet, 0)
    ring_mates = NEAR + (3, -3, FAR, -FAR)
    for s in ring_mates:
        pl.semaphore_signal(barrier, inc=1, device_id=ring_device(s), device_id_type=MESH)

    anchors = anchors_ref[...]
    held = anchors.shape[0]
    blk = held // own
    row = lax.broadcasted_iota(jnp.int32, (pair * own, held), 0)
    col = lax.broadcasted_iota(jnp.int32, (pair * own, held), 1)

    def pick(place):
        wanted = (row % own) * blk + place * pair + row // own
        return dot(jnp.where(col == wanted, 1.0, 0.0).astype(BF), anchors).astype(BF)

    pair_out[...] = pick(me + 1 - 2 * core).reshape(pair_out.shape)
    mine[core] = pick(me).reshape(pair_out.shape)
    pl.semaphore_wait(barrier, size - 1 + len(ring_mates))

    pair_copy = pltpu.make_async_remote_copy(
        src_ref=pair_out,
        dst_ref=mine.at[core],
        send_sem=pair_sems.at[0],
        recv_sem=pair_sems.at[1],
        device_id={"dev": dev + 1 - 2 * core},
        device_id_type=MESH,
    )
    pair_copy.start()
    own_ids = lambda partner: ids_ref
    plane_each(1, size, start, own_ids, all_ids, ids_sems)
    all_ids[me] = ids_ref[...]

    row_iota = lax.broadcasted_iota(jnp.int32, (rows, lanes), 0)
    mix = mix_ref[...]

    def prepare(step, carry):
        for u in range(UNROLL):
            c = step * UNROLL + u
            ot = jnp.where(row_iota == rows_ref[pl.ds(c, 1), :], 1.0, 0.0).astype(BF)
            ot_buf[c] = ot
            pt_buf[c] = dot(ot, mix).astype(BF)
        return carry

    member = jnp.where(
        lax.broadcasted_iota(jnp.int32, (lanes, per), 0) // fields
        == lax.broadcasted_iota(jnp.int32, (lanes, per), 1),
        1.0,
        0.0,
    ).astype(F32)
    total_buf[...] = jnp.zeros(total_buf.shape, F32)
    pair_copy.wait()

    def gather_start():
        zm, zp = (z + length - FAR) % length, (z + FAR) % length
        own_copies = [
            ring_copy(n, s, mine, every.at[z], gather_sems) for n, s in enumerate((FAR, -FAR) + NEAR)
        ]
        low = [ring_copy(6 + n, s, every.at[zm], every.at[zm], gather_sems) for n, s in enumerate(NEAR)]
        low.append(ring_copy(10, 3, every.at[zm, 0], every.at[zm, 0], gather_sems))
        high = [ring_copy(11 + n, s, every.at[zp], every.at[zp], gather_sems) for n, s in enumerate(NEAR)]
        high.append(ring_copy(15, -3, every.at[zp, 1], every.at[zp, 1], gather_sems))
        for copy in own_copies:
            copy.start()
        every[z] = mine[...]
        return own_copies, low, high

    def gather_end(own_copies, low, high):
        own_copies[0].wait_recv()
        for copy in low:
            copy.start()
        own_copies[1].wait_recv()
        for copy in high:
            copy.start()
        for copy in own_copies[2:] + low + high:
            copy.wait_recv()
        for copy in own_copies + low + high:
            copy.wait_send()

    def reduce():
        def near(k):
            return (z + k + 2 * length) % length

        copies = []
        for a, s in enumerate(NEAR):
            copies.append(ring_copy(a, s, sums.at[near(s - FAR)], reduce_in.at[a], reduce_sems))
            copies.append(ring_copy(4 + a, s, sums.at[near(s + FAR)], reduce_in.at[4 + a], reduce_sems))
        copies.append(ring_copy(8, -3, sums.at[near(8), 0], half_in.at[0], reduce_sems))
        copies.append(ring_copy(9, 3, sums.at[near(8), 1], half_in.at[1], reduce_sems))
        direct = [
            ring_copy(10 + a, s, sums.at[near(s)], reduce_in.at[8 + a], reduce_sems)
            for a, s in enumerate(NEAR)
        ]
        for copy in copies + direct:
            copy.start()
        for copy in copies:
            copy.wait_recv()
        far = []
        for h, s in ((0, -FAR), (1, FAR)):
            value = sums[near(s)].astype(F32)
            for a in range(4):
                value = value + reduce_in[4 * h + a].astype(F32)
            collect_out[h, 1 - h] = value[1 - h].astype(BF)
            collect_out[h, h] = (value[h] + half_in[h].astype(F32)).astype(BF)
            far.append(ring_copy(14 + h, s, collect_out.at[h], reduce_in.at[12 + h], reduce_sems))
            far[h].start()
        grad = sums[z].astype(F32)
        for a, copy in enumerate(direct):
            copy.wait_recv()
            grad = grad + reduce_in[8 + a].astype(F32)
        for h, copy in enumerate(far):
            copy.wait_recv()
            grad = grad + reduce_in[12 + h].astype(F32)
        for copy in copies + direct + far:
            copy.wait_send()
        return grad

    fore_source = lambda partner: fore_out.at[partner]
    back_source = lambda partner: back_out.at[partner]

    def part_of(q, sign):
        return (me // PART + sign * q + parts) % parts

    def forward():
        for q in range(parts):
            part = part_of(q, 1)
            picks = picker[pl.ds(pl.multiple_of(part * PART * span, PART * span), PART * span), :]
            for i in range(pair):
                picked = dot(picks, every[:, :, i].reshape(blocks, width)).astype(BF)
                fore_out[pl.ds(part * PART, PART), i] = picked.reshape(PART, span, width)
            plane_each(max(1, q * PART), (q + 1) * PART, start, fore_source, fore_in, fore_sems)
        fore_in[me] = fore_out[me]
        depth = PART * pair * span
        table = jnp.zeros((rows, width), F32)
        for q in range(parts):
            plane_each(max(1, q * PART), (q + 1) * PART, wait_recv, fore_source, fore_in, fore_sems)
            part = part_of(q, -1)
            weights = weights_ref[:, pl.ds(pl.multiple_of(part * depth, depth), depth)]
            table = table + dot(weights, fore_in[pl.ds(part * PART, PART)].reshape(depth, width))
        table_buf[...] = table.astype(BF)
        plane_each(1, size, wait_send, fore_source, fore_in, fore_sems)

    def interact():
        table = table_buf[...]
        gram_high, gram_low = split(dot(table, table, ((1,), (1,))))
        gram = jnp.concatenate([gram_high, gram_low], axis=0)

        def first(step, carry):
            for u in range(UNROLL):
                c = step * UNROLL + u
                q = dot(gram, ot_buf[c])
                q = q[:rows] + q[rows:]
                z_buf[pl.ds(c, 1), :] = jnp.sum(q * pt_buf[c].astype(F32), axis=0, keepdims=True)
            return carry

        lax.fori_loop(0, chunks // UNROLL, first, 0)
        score = 0.5 * dot(z_buf[...], member, precision=HIGH)
        score_ref[...] = score
        slope = 1.0 / (1.0 + jnp.exp(-score)) - labels_ref[...].astype(F32)
        z_buf[...] = dot(slope, member, ((1,), (1,)), precision=HIGH)

        def second(step, total):
            for u in range(UNROLL):
                c = step * UNROLL + u
                w = (z_buf[pl.ds(c, 1), :] * pt_buf[c].astype(F32)).astype(BF)
                total = total + dot(w, ot_buf[c], ((1,), (1,)))
            return total

        total = lax.fori_loop(0, chunks // UNROLL, second, jnp.zeros((rows, rows), F32))
        high, low = split(total)
        return (dot(high, table) + dot(low, table)).astype(BF)

    def backward(row_grad):
        depth = PART * pair * span
        for q in range(parts):
            part = part_of(q, 1)
            weights = weights_t_ref[pl.ds(pl.multiple_of(part * depth, depth), depth), :]
            back_out[pl.ds(part * PART, PART)] = (
                dot(weights, row_grad).astype(BF).reshape(PART, pair, span, width)
            )
            plane_each(max(1, q * PART), (q + 1) * PART, start, back_source, back_in, back_sems)
        back_in[me] = back_out[me]
        depth = PART * span
        for q in range(parts):
            plane_each(max(1, q * PART), (q + 1) * PART, wait_recv, back_source, back_in, back_sems)
            part = part_of(q, -1)
            places = placer[:, pl.ds(pl.multiple_of(part * depth, depth), depth)]
            for i in range(pair):
                value = dot(places, back_in[pl.ds(part * PART, PART), i].reshape(depth, width))
                if q:
                    value = value + acc_buf[i]
                if q < parts - 1:
                    acc_buf[i] = value
                else:
                    sums[:, :, i] = value.astype(BF).reshape(length, 2, own, width)
        plane_each(1, size, wait_send, back_source, back_in, back_sems)

    def one_step(step, carry):
        pending = gather_start()

        @pl.when(step == 0)
        def _():
            lax.fori_loop(0, chunks // UNROLL, prepare, 0)
            plane_each(1, size, wait_recv, own_ids, all_ids, ids_sems)
            plane_each(1, size, wait_send, own_ids, all_ids, ids_sems)
            quarter = lax.broadcasted_iota(jnp.int32, (1, 128), 1) // span
            block_iota = lax.broadcasted_iota(jnp.int32, (blocks, 128), 0)
            together = 128 // span
            for t in range(size // together):
                line = all_ids[t * together, 0:1, :]
                for u in range(1, together):
                    line = jnp.where(quarter == u, all_ids[t * together + u, 0:1, :], line)
                hot = jnp.where(block_iota == line, 1.0, 0.0)
                placer[:, t * 128 : (t + 1) * 128] = hot.astype(BF)
                picker[t * 128 : (t + 1) * 128, :] = hot.T.astype(BF)

        gather_end(*pending)
        forward()
        backward(interact())
        grad = reduce()
        total_buf[...] = total_buf[...] + grad
        mine[...] = (mine[...].astype(F32) - grad).astype(BF)
        return carry

    lax.fori_loop(0, STEPS, one_step, 0)

    last_out[...] = (-total_buf[...]).astype(BF)
    last_source = lambda partner: last_out.at[partner % 2]
    plane_each(1, size, start, last_source, last_in, last_sems)
    last_in[me] = last_out[core]
    source = lax.broadcasted_iota(jnp.int32, (1, held), 1)
    place = (source % own) * blk + source // own
    target = lax.broadcasted_iota(jnp.int32, (held, held), 0)
    order = jnp.where(target == place, 1.0, 0.0).astype(BF)
    plane_each(1, size, wait_recv, last_source, last_in, last_sems)
    update_ref[...] = dot(order, last_in[...].reshape(held, width))
    plane_each(1, size, wait_send, last_source, last_in, last_sems)


def per_device(anchors, coefs, block_cols, block_counts, sample_rows, labels, pair_weights):
    length = lax.axis_size("dev") // 2
    size = lax.axis_size("group") * 2
    rblocks, slots = block_cols.shape
    blk = coefs.shape[1]
    width = anchors.shape[1]
    own = anchors.shape[0] // blk
    span = rblocks * slots
    blocks = length * 2 * own
    pair = blk // size
    rows = rblocks * blk

    live = (jnp.arange(slots)[None, :] < block_counts[:, None]).astype(BF)
    masked = coefs.reshape(rblocks, blk, slots, size, pair) * live[:, None, :, None, None]
    spread = masked[:, :, None] * jnp.eye(rblocks, dtype=BF)[:, None, :, None, None, None]
    weights = spread.transpose(0, 1, 4, 5, 2, 3).reshape(rows, size * pair * span)

    fields = pair_weights.shape[0]
    off = pair_weights * (1.0 - jnp.eye(fields, dtype=F32))
    sym = (off + off.T).astype(BF)
    per = 256 // fields
    mix = jnp.kron(jnp.eye(per, dtype=BF), sym)
    row_ids = sample_rows.reshape(-1, per * fields)
    targets = labels.reshape(-1, per)
    chunks, lanes = row_ids.shape
    ids_tile = jnp.broadcast_to(jnp.tile(block_cols.reshape(1, span), (1, 128 // span)), (8, 128))

    chunk = (2, pair, own, width)
    plane_buf = VMEM((size, pair, span, width), BF)
    update, score = pl.pallas_call(
        functools.partial(whole_kernel, size, length),
        out_shape=(
            jax.ShapeDtypeStruct(anchors.shape, F32),
            jax.ShapeDtypeStruct(targets.shape, F32),
        ),
        scratch_shapes=[
            VMEM(chunk, BF),
            VMEM((pair, own, width), BF),
            VMEM((size, 8, 128), jnp.int32),
            VMEM((length,) + chunk, BF),
            VMEM((blocks, size * span), BF),
            VMEM((size * span, blocks), BF),
            VMEM((chunks, rows, lanes), BF),
            VMEM((chunks, rows, lanes), BF),
            VMEM((chunks, lanes), F32),
            VMEM((rows, width), BF),
            plane_buf,
            plane_buf,
            plane_buf,
            plane_buf,
            VMEM((pair, blocks, width), F32),
            VMEM((length,) + chunk, BF),
            VMEM((14,) + chunk, BF),
            VMEM((2, pair, own, width), BF),
            VMEM((2,) + chunk, BF),
            VMEM(chunk, F32),
            VMEM((2, pair, own, width), BF),
            VMEM((size, pair, own, width), BF),
            DMA((2, size)),
            DMA((2, size)),
            DMA((2, size)),
            DMA((2, size)),
            DMA((2, 16)),
            DMA((2, 16)),
            DMA((2,)),
        ],
        compiler_params=pltpu.CompilerParams(
            collective_id=0, has_side_effects=True, vmem_limit_bytes=40 << 20
        ),
    )(anchors, ids_tile, weights, weights.T, row_ids, targets, mix)
    return update, score.reshape(-1)


def solution(mesh):
    return jax.shard_map(
        per_device,
        mesh=mesh,
        in_specs=(
            P("dev", None),
            P(("group", "dev"), None, None),
            P(("group", "dev"), None),
            P(("group", "dev")),
            P(("group", "dev"), None),
            P(("group", "dev")),
            P(),
        ),
        out_specs=(P("dev", None), P(("group", "dev"))),
        check_vma=False,
    )
```

time: 1080 us -> 180 us (0.17)
  waiting for transfers between devices: 600 us -> 0 us
  blocking collectives: 224 us -> 0 us
  local copies, waits for them, and re-layouts: 178 us -> 6.84 us
  Pallas kernels: 0 us -> 170 us
  matrix products: 28 us -> 0 us
  starting transfers between devices: 26.4 us -> 0 us
  between operations: 14.3 us -> 0.77 us
    all_to_all x3 -> x0, waiting for transfers between devices: 379 us -> none  [the longest x2 197 us: build_table(): lax.all_to_all(picked.reshape(holders, depth * blk, width), 'dev', split_...]
    all_to_all x2 -> x0, blocking collectives: 224 us -> none  [the longest x1 196 us: return_grads(): lax.all_to_all(outgoing, 'dev', split_axis=0, concat_axis=0, tiled=True)]
    psum x2 -> x0, waiting for transfers between devices: 221 us -> none  [group_total(): return lax.psum(values, 'group')]
    pallas_call x0 -> x1, Pallas kernels: none -> 170 us  [per_device(): pl.pallas_call(functools.partial(whole_kernel, size, length), out_shape=(...]
    gather x20 -> x0, local copies, waits for them, and re-layouts: 129 us -> none  [the longest x16 120 us: one_group(): vecs = table[rows_now]]
    dot_general x38 -> x0, matrix products: 28 us -> none  [the longest x16 11.2 us: one_group(): jnp.einsum('fg,sgw->sfw', sym, vecs, preferred_element_type=jnp.float32)]
    all_to_all x3 -> x0, starting transfers between devices: 26.2 us -> none  [the longest x2 19.2 us: build_table(): lax.all_to_all(picked.reshape(holders, depth * blk, width), 'dev', split_...]
    another operation x4 -> x3, local copies, waits for them, and re-layouts: 14.9 us -> 0.85 us  [per_device(): jnp.tile(block_cols.reshape(1, span), (1, 128 // span))]
  transfers between devices with their start and end apart: 5 -> 0, of which waited for: 5 -> 0; matrix products, arithmetic and copies ran while one was open for 0% -> 0% of each run, Pallas kernels for 0% -> 0%
where the time goes in v2:
time: 180 us
  Pallas kernels  170 us (94%)
  local copies, waits for them, and re-layouts  6.84 us (4%)
  other arithmetic  2.24 us (1%)
    pallas_call x1, Pallas kernels, per_device(): pl.pallas_call(functools.partial(whole_kernel, size, length), out_shape=(...  170 us

profile of v2, /device:TPU:1, one launch (start us, length us, event | category | flops | bytes accessed | tf_op | source)
XLA Modules:
  0.0 180.0 jit_solution(17000564314494078931)
XLA Ops:
  0.6 0.0 copy-start.3
  0.6 0.8 tile.10
  1.4 0.7 compare_convert_fusion.1
  2.1 0.1 tile.12
  2.2 0.0 copy-done.3
  2.2 0.0 copy-start.2
  2.3 0.1 copy.16
  2.3 0.0 copy-start.4
  2.4 0.7 copy-done.4
  3.0 0.1 reshape.76.labels_ref
  3.1 0.0 copy-done.2
  3.1 0.1 copy.15
  3.3 0.1 reshape.75.rows_ref
  3.4 0.1 broadcast_multiply_fusion.1
  3.5 0.0 copy-start.1
  3.5 0.4 mul.70.mix_ref
  3.9 0.6 copy-done.1
  4.5 0.3 copy.13
  4.7 0.5 multiply_bitcast_fusion
  5.3 0.5 copy.14
  5.8 0.8 broadcast_multiply_fusion
  6.7 0.5 mul.65
  7.2 0.0 copy-start
  7.2 0.2 copy.17.weights_ref
  7.4 0.8 copy-done
  8.2 170.1 %shard_map.86 = (f32[1024,256]{1,0:T(8,128)S(1)}, f32[64,8]{1,0:T(8,128)S(1)}) custom-call(bf16[1024,256]{1,0:T(8,128)(2,1)S(1)} %copy-done, s32[8,128]{1,0:T(8,128)S(1)} %broadcast_in_dim.4.ids_ref, bf16[128,2048]{1,0:T(8,128)(2,1)S(1)} %copy.17.weights_ref, bf16[2048,128]{1,0:T(8,128)(2,1)S(1)} %bitcast.12, s32[64,256]{1,0:T(8,128)S(1)} %reshape.75.rows_ref, ...), custom_call_target="tpu_custom_call" | custom-call | tf_op jit(solution)/shard_map/pallas_call | solution.py:408
  178.4 0.7 reshape.77
  179.0 1.0 copy.19
  (6 shorter events, 0.0 us)
Async XLA Ops:
  0.6 1.6 copy-start.3
  2.2 0.9 copy-start.2
  2.3 0.7 copy-start.4
  3.5 1.0 copy-start.1
  7.2 1.0 copy-start

commit v3 on v2

v3 whole, which is shorter than its diff:
```python
import functools

import jax
import jax.numpy as jnp
from jax import lax
from jax.experimental import pallas as pl
from jax.experimental.pallas import tpu as pltpu
from jax.sharding import PartitionSpec as P

BF = jnp.bfloat16
F32 = jnp.float32
HIGH = lax.Precision.HIGHEST
MESH = pl.DeviceIdType.MESH
VMEM = pltpu.VMEM
DMA = pltpu.SemaphoreType.DMA
UNROLL = 8
NEAR = (1, -1, 2, -2)
FAR = 5
STEPS = 2
PART = 8


def dot(a, b, dims=((1,), (0,)), precision=None):
    return lax.dot_general(a, b, (dims, ((), ())), precision=precision, preferred_element_type=F32)


def split(x):
    high = x.astype(BF)
    return high, (x - high.astype(F32)).astype(BF)


def whole_kernel(
    size,
    length,
    counts_ref,
    anchors_ref,
    coefs_ref,
    cols_ref,
    rows_ref,
    labels_ref,
    pairs_ref,
    update_ref,
    score_ref,
    mine,
    pair_out,
    ids_out,
    all_ids,
    every,
    placer,
    picker,
    weights,
    weights_t,
    rows_buf,
    ot_buf,
    pt_buf,
    z_buf,
    table_buf,
    fore_out,
    fore_in,
    back_out,
    back_in,
    acc_buf,
    sums,
    reduce_in,
    half_in,
    collect_out,
    total_buf,
    last_out,
    last_in,
    fore_sems,
    back_sems,
    gather_sems,
    reduce_sems,
    pair_sems,
):
    group, dev = lax.axis_index("group"), lax.axis_index("dev")
    core, z = dev % 2, dev // 2
    me = group * 2 + core
    parts = size // PART
    pair, _, own, width = mine.shape
    span = fore_out.shape[2]
    blocks = placer.shape[0]
    rows = table_buf.shape[0]
    rblocks, blk, deep = coefs_ref.shape
    slots = deep // blk
    chunks, lanes = rows_buf.shape
    per = labels_ref.shape[1]
    fields = lanes // per

    def iota(shape, dim):
        return lax.broadcasted_iota(jnp.int32, shape, dim)

    def hot(mask):
        return jnp.where(mask, 1.0, 0.0).astype(BF)

    def partner_of(n):
        return ((me // PART + n // PART) % parts) * PART + (me % PART + n % PART) % PART

    def plane_device(partner):
        return {"group": partner // 2, "dev": z * 2 + partner % 2}

    def plane_copy(n, i, source, target, sems):
        partner = partner_of(n)
        return pltpu.make_async_remote_copy(
            src_ref=source(partner),
            dst_ref=target.at[me],
            send_sem=sems.at[0, i * size + n],
            recv_sem=sems.at[1, i * size + n],
            device_id=plane_device(partner),
            device_id_type=MESH,
        )

    def plane_each(first, last, act, i, source, target, sems):
        def one(n, carry):
            act(plane_copy(n, i, source, target, sems))
            return carry

        lax.fori_loop(first, last, one, 0)

    def start(copy):
        copy.start()

    def wait_recv(copy):
        copy.wait_recv()

    def wait_send(copy):
        copy.wait_send()

    def ring_device(s):
        return {"dev": (dev + 2 * s + 2 * length) % (2 * length)}

    def ring_copy(n, i, s, source, target, sems):
        return pltpu.make_async_remote_copy(
            src_ref=source,
            dst_ref=target,
            send_sem=sems.at[0, i * 16 + n],
            recv_sem=sems.at[1, i * 16 + n],
            device_id=ring_device(s),
            device_id_type=MESH,
        )

    def near(k):
        return (z + k + 2 * length) % length

    barrier = pltpu.get_barrier_semaphore()

    def greet(n, carry):
        pl.semaphore_signal(
            barrier, inc=1, device_id=plane_device(partner_of(n)), device_id_type=MESH
        )
        return carry

    ring_mates = NEAR + (3, -3, FAR, -FAR)
    for s in ring_mates:
        pl.semaphore_signal(barrier, inc=1, device_id=ring_device(s), device_id_type=MESH)
    lax.fori_loop(1, size, greet, 0)

    anchors = anchors_ref[...]
    held = anchors.shape[0]
    row = iota((pair * own, held), 0)
    col = iota((pair * own, held), 1)

    def pick(place):
        wanted = (row % own) * blk + place * pair + row // own
        return dot(hot(col == wanted), anchors).astype(BF).reshape(pair_out.shape)

    pair_out[...] = pick(me + 1 - 2 * core)
    kept = pick(me)
    for i in range(pair):
        mine[i, core] = kept[i]
    line = jnp.concatenate([cols_ref[b : b + 1, :] for b in range(rblocks)] * (128 // span), axis=1)
    ids_out[...] = jnp.broadcast_to(line, ids_out.shape)
    pl.semaphore_wait(barrier, size - 1 + len(ring_mates))

    pair_copies = [
        pltpu.make_async_remote_copy(
            src_ref=pair_out.at[i],
            dst_ref=mine.at[i, core],
            send_sem=pair_sems.at[0, i],
            recv_sem=pair_sems.at[1, i],
            device_id={"dev": dev + 1 - 2 * core},
            device_id_type=MESH,
        )
        for i in range(pair)
    ]
    for copy in pair_copies:
        copy.start()
    own_ids = lambda partner: ids_out
    plane_each(1, size, start, 0, own_ids, all_ids, back_sems)
    all_ids[me] = ids_out[...]

    def gather_own(i):
        return [
            ring_copy(n, i, s, mine.at[i], every.at[i, z], gather_sems)
            for n, s in enumerate((FAR, -FAR) + NEAR)
        ]

    def gather_on(i, h):
        held_at = near(-FAR if h == 0 else FAR)
        piece = every.at[i, held_at]
        copies = [ring_copy(6 + 5 * h + n, i, s, piece, piece, gather_sems) for n, s in enumerate(NEAR)]
        half = every.at[i, held_at, h]
        copies.append(ring_copy(10 + 5 * h, i, 3 if h == 0 else -3, half, half, gather_sems))
        return copies

    def gather_start(i):
        for copy in gather_own(i):
            copy.start()
        every[i, z] = mine[i]

    def gather_forward(i):
        for h in (0, 1):
            gather_own(i)[h].wait_recv()
            for copy in gather_on(i, h):
                copy.start()

    def gather_end(i):
        for copy in gather_own(i)[2:] + gather_on(i, 0) + gather_on(i, 1):
            copy.wait_recv()

    def gather_sent():
        for i in range(pair):
            for copy in gather_own(i) + gather_on(i, 0) + gather_on(i, 1):
                copy.wait_send()

    for i in range(pair):
        pair_copies[i].wait()
        gather_start(i)

    member = jnp.where(
        iota((lanes, per), 0) // fields == iota((lanes, per), 1), 1.0, 0.0
    ).astype(F32)
    total_buf[...] = jnp.zeros(total_buf.shape, F32)
    off = jnp.where(iota((fields, fields), 0) == iota((fields, fields), 1), 0.0, pairs_ref[...])
    sym = (off + off.T).astype(BF)
    repeat = hot(iota((lanes, fields), 0) % fields == iota((lanes, fields), 1))
    mix = dot(dot(repeat, sym).astype(BF), repeat, ((1,), (1,)))
    mix = jnp.where(iota((lanes, lanes), 0) // fields == iota((lanes, lanes), 1) // fields, mix, 0.0)
    mix = mix.astype(BF)
    rows_buf[...] = jnp.concatenate(
        [rows_ref[pl.ds(u, chunks, stride=per), :] for u in range(per)], axis=1
    )
    row_iota = iota((rows, lanes), 0)

    def prepare(step, carry):
        for u in range(UNROLL):
            c = step * UNROLL + u
            ot = hot(row_iota == rows_buf[pl.ds(c, 1), :])
            ot_buf[c] = ot
            pt_buf[c] = dot(ot, mix).astype(BF)
        return carry

    lax.fori_loop(0, chunks // UNROLL, prepare, 0)
    for i in range(pair):
        gather_forward(i)

    plane_each(1, size, wait_recv, 0, own_ids, all_ids, back_sems)
    plane_each(1, size, wait_send, 0, own_ids, all_ids, back_sems)
    quarter = iota((1, 128), 1) // span
    block_iota = iota((blocks, 128), 0)
    together = 128 // span
    for t in range(size // together):
        line = all_ids[t * together, 0:1, :]
        for u in range(1, together):
            line = jnp.where(quarter == u, all_ids[t * together + u, 0:1, :], line)
        found = jnp.where(block_iota == line, 1.0, 0.0)
        placer[:, t * 128 : (t + 1) * 128] = found.astype(BF)
        picker[t * 128 : (t + 1) * 128, :] = found.T.astype(BF)

    flat = coefs_ref[...].reshape(rows, deep)
    tile = 256
    for t in range(weights.shape[1] // tile):
        n = iota((1, tile), 1) + t * tile
        slot, block = n % slots, (n // slots) % rblocks
        offset = (n // span) % size * pair + n // (span * size)
        order = hot(iota((deep, tile), 0) == slot * blk + offset)
        bound = jnp.where(block == 0, counts_ref[0], counts_ref[1])
        block = jnp.where(slot < bound, block, rblocks)
        value = jnp.where(iota((rows, tile), 0) // blk == block, dot(flat, order), 0.0)
        weights[:, t * tile : (t + 1) * tile] = value.astype(BF)
        weights_t[t * tile : (t + 1) * tile, :] = value.T.astype(BF)

    def part_of(q, sign):
        return (me // PART + sign * q + parts) % parts

    depth = PART * span

    def from_part(base, part):
        return pl.ds(pl.multiple_of(base + part * depth, depth), depth)

    def fore(act, i, q):
        first, last = max(1, q * PART), (q + 1) * PART
        plane_each(first, last, act, i, lambda partner: fore_out.at[i, partner], fore_in.at[i], fore_sems)

    def back(act, i, q):
        first, last = max(1, q * PART), (q + 1) * PART
        plane_each(first, last, act, i, lambda partner: back_out.at[i, partner], back_in.at[i], back_sems)

    def final(act, i):
        plane_each(1, size, act, i, lambda partner: last_out.at[i, partner % 2], last_in.at[i], fore_sems)

    def forward():
        for i in range(pair):
            gather_end(i)
            for q in range(parts):
                part = part_of(q, 1)
                picks = picker[from_part(0, part), :]
                picked = dot(picks, every[i].reshape(blocks, width)).astype(BF)
                fore_out[i, pl.ds(part * PART, PART)] = picked.reshape(PART, span, width)
                fore(start, i, q)
            fore_in[i, me] = fore_out[i, me]
        gather_sent()
        table = jnp.zeros((rows, width), F32)
        for i in range(pair):
            for q in range(parts):
                fore(wait_recv, i, q)
                part = part_of(q, -1)
                got = fore_in[i, pl.ds(part * PART, PART)].reshape(depth, width)
                table = table + dot(weights[:, from_part(i * size * span, part)], got)
        table_buf[...] = table.astype(BF)

    def interact():
        table = table_buf[...]
        gram_high, gram_low = split(dot(table, table, ((1,), (1,))))
        gram = jnp.concatenate([gram_high, gram_low], axis=0)

        def first(step, carry):
            for u in range(UNROLL):
                c = step * UNROLL + u
                q = dot(gram, ot_buf[c])
                q = q[:rows] + q[rows:]
                z_buf[pl.ds(c, 1), :] = jnp.sum(q * pt_buf[c].astype(F32), axis=0, keepdims=True)
            return carry

        lax.fori_loop(0, chunks // UNROLL, first, 0)
        score = 0.5 * dot(z_buf[...], member, precision=HIGH)
        score_ref[...] = score
        slope = 1.0 / (1.0 + jnp.exp(-score)) - labels_ref[...].astype(F32)
        z_buf[...] = dot(slope, member, ((1,), (1,)), precision=HIGH)

        def second(step, total):
            for u in range(UNROLL):
                c = step * UNROLL + u
                w = (z_buf[pl.ds(c, 1), :] * pt_buf[c].astype(F32)).astype(BF)
                total = total + dot(w, ot_buf[c], ((1,), (1,)))
            return total

        total = lax.fori_loop(0, chunks // UNROLL, second, jnp.zeros((rows, rows), F32))
        high, low = split(total)
        return (dot(high, table) + dot(low, table)).astype(BF)

    def reduce_copies(i):
        held_sums, taken = sums.at[i], reduce_in.at[i]
        copies = []
        for a, s in enumerate(NEAR):
            copies.append(ring_copy(a, i, s, held_sums.at[near(s - FAR)], taken.at[a], reduce_sems))
            copies.append(ring_copy(4 + a, i, s, held_sums.at[near(s + FAR)], taken.at[4 + a], reduce_sems))
        copies.append(ring_copy(8, i, -3, held_sums.at[near(8), 0], half_in.at[i, 0], reduce_sems))
        copies.append(ring_copy(9, i, 3, held_sums.at[near(8), 1], half_in.at[i, 1], reduce_sems))
        direct = [
            ring_copy(10 + a, i, s, held_sums.at[near(s)], taken.at[8 + a], reduce_sems)
            for a, s in enumerate(NEAR)
        ]
        far = [
            ring_copy(14 + h, i, s, collect_out.at[i, h], taken.at[12 + h], reduce_sems)
            for h, s in ((0, -FAR), (1, FAR))
        ]
        return copies, direct, far

    def backward(row_grad):
        for i in range(pair):
            for q in range(parts):
                part = part_of(q, 1)
                value = dot(weights_t[from_part(i * size * span, part), :], row_grad).astype(BF)
                back_out[i, pl.ds(part * PART, PART)] = value.reshape(PART, span, width)
                back(start, i, q)
            back_in[i, me] = back_out[i, me]
        for i in range(pair):
            for q in range(parts):
                fore(wait_send, i, q)
        for i in range(pair):
            for q in range(parts):
                back(wait_recv, i, q)
                part = part_of(q, -1)
                got = back_in[i, pl.ds(part * PART, PART)].reshape(depth, width)
                value = dot(placer[:, from_part(0, part)], got)
                if q:
                    value = value + acc_buf[...]
                if q < parts - 1:
                    acc_buf[...] = value
                else:
                    sums[i] = value.astype(BF).reshape(length, 2, own, width)
            copies, direct, _ = reduce_copies(i)
            for copy in copies + direct:
                copy.start()

    def collect(i):
        copies, _, far = reduce_copies(i)
        for copy in copies:
            copy.wait_recv()
        for h, s in ((0, -FAR), (1, FAR)):
            value = sums[i, near(s)].astype(F32)
            for a in range(4):
                value = value + reduce_in[i, 4 * h + a].astype(F32)
            collect_out[i, h, 1 - h] = value[1 - h].astype(BF)
            collect_out[i, h, h] = (value[h] + half_in[i, h].astype(F32)).astype(BF)
            far[h].start()

    def reduced(i):
        _, direct, far = reduce_copies(i)
        grad = sums[i, z].astype(F32)
        for copy in direct + far:
            copy.wait_recv()
        for a in range(6):
            grad = grad + reduce_in[i, 8 + a].astype(F32)
        return grad

    def one_step(step, carry):
        @pl.when(step > 0)
        def _():
            for i in range(pair):
                gather_forward(i)

        forward()
        backward(interact())
        for i in range(pair):
            collect(i)
        for i in range(pair):
            grad = reduced(i)
            total = total_buf[i] + grad
            total_buf[i] = total
            mine[i] = (mine[i].astype(F32) - grad).astype(BF)

            @pl.when(step < STEPS - 1)
            def _():
                gather_start(i)

            @pl.when(step == STEPS - 1)
            def _():
                last_out[i] = (-total).astype(BF)
                final(start, i)
                last_in[i, me] = last_out[i, core]

        for i in range(pair):
            copies, direct, far = reduce_copies(i)
            for copy in copies + direct + far:
                copy.wait_send()
            for q in range(parts):
                back(wait_send, i, q)
        return carry

    lax.fori_loop(0, STEPS, one_step, 0)

    source = iota((1, held), 1)
    place = (source % own) * blk + (source // own) % size * pair + source // (own * size)
    order = hot(iota((held, held), 0) == place)
    for i in range(pair):
        final(wait_recv, i)
    update_ref[...] = dot(order, last_in[...].reshape(held, width))
    for i in range(pair):
        final(wait_send, i)


def per_device(anchors, coefs, block_cols, block_counts, sample_rows, labels, pair_weights):
    length = lax.axis_size("dev") // 2
    size = lax.axis_size("group") * 2
    rblocks, slots = block_cols.shape
    blk = coefs.shape[1]
    width = anchors.shape[1]
    own = anchors.shape[0] // blk
    span = rblocks * slots
    blocks = length * 2 * own
    pair = blk // size
    rows = rblocks * blk
    samples, fields = sample_rows.shape
    lanes = 256
    per = lanes // fields
    chunks = samples // per
    targets = labels.reshape(chunks, per)

    chunk = (2, own, width)
    plane_buf = VMEM((pair, size, span, width), BF)
    vmem = pl.BlockSpec(memory_space=VMEM)
    update, score = pl.pallas_call(
        functools.partial(whole_kernel, size, length),
        out_shape=(
            jax.ShapeDtypeStruct(anchors.shape, F32),
            jax.ShapeDtypeStruct(targets.shape, F32),
        ),
        in_specs=[pl.BlockSpec(memory_space=pltpu.SMEM)] + [vmem] * 6,
        out_specs=(vmem, vmem),
        scratch_shapes=[
            VMEM((pair,) + chunk, BF),
            VMEM((pair, own, width), BF),
            VMEM((8, 128), jnp.int32),
            VMEM((size, 8, 128), jnp.int32),
            VMEM((pair, length) + chunk, BF),
            VMEM((blocks, size * span), BF),
            VMEM((size * span, blocks), BF),
            VMEM((rows, size * pair * span), BF),
            VMEM((size * pair * span, rows), BF),
            VMEM((chunks, lanes), jnp.int32),
            VMEM((chunks, rows, lanes), BF),
            VMEM((chunks, rows, lanes), BF),
            VMEM((chunks, lanes), F32),
            VMEM((rows, width), BF),
            plane_buf,
            plane_buf,
            plane_buf,
            plane_buf,
            VMEM((blocks, width), F32),
            VMEM((pair, length) + chunk, BF),
            VMEM((pair, 14) + chunk, BF),
            VMEM((pair, 2, own, width), BF),
            VMEM((pair, 2) + chunk, BF),
            VMEM((pair,) + chunk, F32),
            VMEM((pair, 2, own, width), BF),
            VMEM((pair, size, own, width), BF),
            DMA((2, pair * size)),
            DMA((2, pair * size)),
            DMA((2, pair * 16)),
            DMA((2, pair * 16)),
            DMA((2, pair)),
        ],
        compiler_params=pltpu.CompilerParams(
            collective_id=0, has_side_effects=True, vmem_limit_bytes=40 << 20
        ),
    )(block_counts, anchors, coefs, block_cols, sample_rows, targets, pair_weights)
    return update, score.reshape(-1)


def solution(mesh):
    return jax.shard_map(
        per_device,
        mesh=mesh,
        in_specs=(
            P("dev", None),
            P(("group", "dev"), None, None),
            P(("group", "dev"), None),
            P(("group", "dev")),
            P(("group", "dev"), None),
            P(("group", "dev")),
            P(),
        ),
        out_specs=(P("dev", None), P(("group", "dev"))),
        check_vma=False,
    )
```

time: 180 us -> 152 us (0.84)
  Pallas kernels: 170 us -> 147 us
  local copies, waits for them, and re-layouts: 6.84 us -> 4.48 us
  other arithmetic: 2.24 us -> 0 us
    pallas_call x1, Pallas kernels: 170 us -> 147 us  [per_device(): pl.pallas_call(functools.partial(whole_kernel, size, length), out_shape=(...]
where the time goes in v3:
time: 152 us
  Pallas kernels  147 us (97%)
  local copies, waits for them, and re-layouts  4.48 us (3%)
    pallas_call x1, Pallas kernels, per_device(): pl.pallas_call(functools.partial(whole_kernel, size, length), out_shape=(...  147 us

profile of v3, /device:TPU:1, one launch (start us, length us, event | category | flops | bytes accessed | tf_op | source)
XLA Modules:
  0.0 152.0 jit_solution(9421147185573224419)
XLA Ops:
  0.6 0.0 copy-start.1
  0.6 0.8 reshape.10.labels_ref
  1.5 0.0 copy-start.2
  1.5 0.0 copy-start.3
  1.5 0.0 copy-start.4
  1.5 1.0 copy.10.rows_ref
  2.5 0.0 copy-done.1
  2.5 0.0 copy-done.2
  2.5 0.0 copy-done.3
  2.5 0.0 copy-done.4
  2.5 0.0 copy-start
  2.5 1.0 copy-done
  3.6 146.8 %shard_map.86 = (f32[1024,256]{1,0:T(8,128)S(1)}, f32[64,8]{1,0:T(8,128)S(1)}) custom-call(s32[2]{0:T(128)S(1)} %copy-done.4, bf16[1024,256]{1,0:T(8,128)(2,1)S(1)} %copy-done, bf16[2,64,1024]{2,1,0:T(8,128)(2,1)S(1)} %copy-done.1, s32[2,16]{1,0:T(2,128)S(1)} %copy-done.3, s32[512,32]{1,0:T(8,128)S(1)} %copy.10.rows_ref, s32[64,8]{1,0:T(8,128)S(1)} %reshape.10.labels_ref, ...), custom_call_target="tpu_custom_call" | custom-call | tf_op jit(solution)/shard_map/pallas_call | solution.py:484
  150.3 0.7 reshape.11
  151.0 1.0 copy.12
Async XLA Ops:
  0.6 1.8 %copy-start.1 = (bf16[2,64,1024]{2,1,0:T(8,128)(2,1)S(1)}, bf16[2,64,1024]{2,1,0:T(8,128)(2,1)}, u32[]{:S(2)}) copy-start(bf16[2,64,1024]{2,1,0:T(8,128)(2,1)} %coefs_ref.1) | copy-start | bytes 786436
  1.5 1.0 copy-start.2
  1.5 1.0 copy-start.3
  1.5 1.0 copy-start.4
  2.5 1.0 copy-start

commit v4 on v3

--- a/solution.py
+++ b/solution.py
@@ -9,7 +9,6 @@
 
 BF = jnp.bfloat16
 F32 = jnp.float32
-HIGH = lax.Precision.HIGHEST
 MESH = pl.DeviceIdType.MESH
 VMEM = pltpu.VMEM
 DMA = pltpu.SemaphoreType.DMA
@@ -20,8 +19,8 @@
 PART = 8
 
 
-def dot(a, b, dims=((1,), (0,)), precision=None):
-    return lax.dot_general(a, b, (dims, ((), ())), precision=precision, preferred_element_type=F32)
+def dot(a, b, dims=((1,), (0,))):
+    return lax.dot_general(a, b, (dims, ((), ())), preferred_element_type=F32)
 
 
 def split(x):
@@ -93,29 +92,38 @@
     def hot(mask):
         return jnp.where(mask, 1.0, 0.0).astype(BF)
 
-    def partner_of(n):
-        return ((me // PART + n // PART) % parts) * PART + (me % PART + n % PART) % PART
+    my_part, my_place = me // PART, me % PART
+    plane_base = z * 2
+
+    def part_of(q):
+        return lax.rem(my_part + (q + parts), parts)
 
     def plane_device(partner):
-        return {"group": partner // 2, "dev": z * 2 + partner % 2}
-
-    def plane_copy(n, i, source, target, sems):
-        partner = partner_of(n)
-        return pltpu.make_async_remote_copy(
-            src_ref=source(partner),
-            dst_ref=target.at[me],
-            send_sem=sems.at[0, i * size + n],
-            recv_sem=sems.at[1, i * size + n],
-            device_id=plane_device(partner),
-            device_id_type=MESH,
-        )
-
-    def plane_each(first, last, act, i, source, target, sems):
-        def one(n, carry):
-            act(plane_copy(n, i, source, target, sems))
+        return {"group": lax.div(partner, 2), "dev": plane_base + lax.rem(partner, 2)}
+
+    def each_partner(q, act):
+        base = part_of(q) * PART
+
+        def one(j, carry):
+            act(q * PART + j, base + lax.rem(my_place + j, PART))
             return carry
 
-        lax.fori_loop(first, last, one, 0)
+        lax.fori_loop(1 if q == 0 else 0, PART, one, 0)
+
+    def plane_each(q, act, i, source, target, sems):
+        def one(n, partner):
+            act(
+                pltpu.make_async_remote_copy(
+                    src_ref=source(partner),
+                    dst_ref=target.at[me],
+                    send_sem=sems.at[0, i * size + n],
+                    recv_sem=sems.at[1, i * size + n],
+                    device_id=plane_device(partner),
+                    device_id_type=MESH,
+                )
+            )
+
+        each_partner(q, one)
 
     def start(copy):
         copy.start()
@@ -144,16 +152,14 @@
 
     barrier = pltpu.get_barrier_semaphore()
 
-    def greet(n, carry):
-        pl.semaphore_signal(
-            barrier, inc=1, device_id=plane_device(partner_of(n)), device_id_type=MESH
-        )
-        return carry
+    def greet(n, partner):
+        pl.semaphore_signal(barrier, inc=1, device_id=plane_device(partner), device_id_type=MESH)
 
     ring_mates = NEAR + (3, -3, FAR, -FAR)
     for s in ring_mates:
         pl.semaphore_signal(barrier, inc=1, device_id=ring_device(s), device_id_type=MESH)
-    lax.fori_loop(1, size, greet, 0)
+    for q in range(parts):
+        each_partner(q, greet)
 
     anchors = anchors_ref[...]
     held = anchors.shape[0]
@@ -186,14 +192,13 @@
     for copy in pair_copies:
         copy.start()
     own_ids = lambda partner: ids_out
-    plane_each(1, size, start, 0, own_ids, all_ids, back_sems)
+    for q in range(parts):
+        plane_each(q, start, 0, own_ids, all_ids, back_sems)
     all_ids[me] = ids_out[...]
 
-    def gather_own(i):
-        return [
-            ring_copy(n, i, s, mine.at[i], every.at[i, z], gather_sems)
-            for n, s in enumerate((FAR, -FAR) + NEAR)
-        ]
+    def gather_own(i, first=0, last=6):
+        ways = tuple(enumerate((FAR, -FAR) + NEAR))[first:last]
+        return [ring_copy(n, i, s, mine.at[i], every.at[i, z], gather_sems) for n, s in ways]
 
     def gather_on(i, h):
         held_at = near(-FAR if h == 0 else FAR)
@@ -204,18 +209,21 @@
         return copies
 
     def gather_start(i):
-        for copy in gather_own(i):
+        for copy in gather_own(i) if i == 0 else gather_own(i, 0, 2):
             copy.start()
         every[i, z] = mine[i]
 
     def gather_forward(i):
+        if i:
+            for copy in gather_own(i, 2):
+                copy.start()
         for h in (0, 1):
-            gather_own(i)[h].wait_recv()
+            gather_own(i, h, h + 1)[0].wait_recv()
             for copy in gather_on(i, h):
                 copy.start()
 
     def gather_end(i):
-        for copy in gather_own(i)[2:] + gather_on(i, 0) + gather_on(i, 1):
+        for copy in gather_own(i, 2) + gather_on(i, 0) + gather_on(i, 1):
             copy.wait_recv()
 
     def gather_sent():
@@ -227,9 +235,7 @@
         pair_copies[i].wait()
         gather_start(i)
 
-    member = jnp.where(
-        iota((lanes, per), 0) // fields == iota((lanes, per), 1), 1.0, 0.0
-    ).astype(F32)
+    member = hot(iota((lanes, per), 0) // fields == iota((lanes, per), 1))
     total_buf[...] = jnp.zeros(total_buf.shape, F32)
     off = jnp.where(iota((fields, fields), 0) == iota((fields, fields), 1), 0.0, pairs_ref[...])
     sym = (off + off.T).astype(BF)
@@ -254,8 +260,9 @@
     for i in range(pair):
         gather_forward(i)
 
-    plane_each(1, size, wait_recv, 0, own_ids, all_ids, back_sems)
-    plane_each(1, size, wait_send, 0, own_ids, all_ids, back_sems)
+    for q in range(parts):
+        plane_each(q, wait_recv, 0, own_ids, all_ids, back_sems)
+        plane_each(q, wait_send, 0, own_ids, all_ids, back_sems)
     quarter = iota((1, 128), 1) // span
     block_iota = iota((blocks, 128), 0)
     together = 128 // span
@@ -280,30 +287,28 @@
         weights[:, t * tile : (t + 1) * tile] = value.astype(BF)
         weights_t[t * tile : (t + 1) * tile, :] = value.T.astype(BF)
 
-    def part_of(q, sign):
-        return (me // PART + sign * q + parts) % parts
-
     depth = PART * span
 
     def from_part(base, part):
         return pl.ds(pl.multiple_of(base + part * depth, depth), depth)
 
     def fore(act, i, q):
-        first, last = max(1, q * PART), (q + 1) * PART
-        plane_each(first, last, act, i, lambda partner: fore_out.at[i, partner], fore_in.at[i], fore_sems)
+        plane_each(q, act, i, lambda partner: fore_out.at[i, partner], fore_in.at[i], fore_sems)
 
     def back(act, i, q):
-        first, last = max(1, q * PART), (q + 1) * PART
-        plane_each(first, last, act, i, lambda partner: back_out.at[i, partner], back_in.at[i], back_sems)
+        plane_each(q, act, i, lambda partner: back_out.at[i, partner], back_in.at[i], back_sems)
 
     def final(act, i):
-        plane_each(1, size, act, i, lambda partner: last_out.at[i, partner % 2], last_in.at[i], fore_sems)
+        for q in range(parts):
+            plane_each(
+                q, act, i, lambda partner: last_out.at[i, lax.rem(partner, 2)], last_in.at[i], fore_sems
+            )
 
     def forward():
         for i in range(pair):
             gather_end(i)
             for q in range(parts):
-                part = part_of(q, 1)
+                part = part_of(q)
                 picks = picker[from_part(0, part), :]
                 picked = dot(picks, every[i].reshape(blocks, width)).astype(BF)
                 fore_out[i, pl.ds(part * PART, PART)] = picked.reshape(PART, span, width)
@@ -314,34 +319,33 @@
         for i in range(pair):
             for q in range(parts):
                 fore(wait_recv, i, q)
-                part = part_of(q, -1)
+                part = part_of(-q)
                 got = fore_in[i, pl.ds(part * PART, PART)].reshape(depth, width)
                 table = table + dot(weights[:, from_part(i * size * span, part)], got)
         table_buf[...] = table.astype(BF)
 
     def interact():
         table = table_buf[...]
-        gram_high, gram_low = split(dot(table, table, ((1,), (1,))))
-        gram = jnp.concatenate([gram_high, gram_low], axis=0)
+        gram = dot(table, table, ((1,), (1,))).astype(BF)
 
         def first(step, carry):
             for u in range(UNROLL):
                 c = step * UNROLL + u
-                q = dot(gram, ot_buf[c])
-                q = q[:rows] + q[rows:]
-                z_buf[pl.ds(c, 1), :] = jnp.sum(q * pt_buf[c].astype(F32), axis=0, keepdims=True)
+                q = dot(gram, ot_buf[c]) * pt_buf[c].astype(F32)
+                z_buf[pl.ds(c, 1), :] = jnp.sum(q, axis=0, keepdims=True)
             return carry
 
         lax.fori_loop(0, chunks // UNROLL, first, 0)
-        score = 0.5 * dot(z_buf[...], member, precision=HIGH)
+        high, low = split(z_buf[...])
+        score = 0.5 * (dot(high, member) + dot(low, member))
         score_ref[...] = score
         slope = 1.0 / (1.0 + jnp.exp(-score)) - labels_ref[...].astype(F32)
-        z_buf[...] = dot(slope, member, ((1,), (1,)), precision=HIGH)
+        z_buf[...] = dot(slope.astype(BF), member, ((1,), (1,)))
 
         def second(step, total):
             for u in range(UNROLL):
                 c = step * UNROLL + u
-                w = (z_buf[pl.ds(c, 1), :] * pt_buf[c].astype(F32)).astype(BF)
+                w = z_buf[pl.ds(c, 1), :].astype(BF) * pt_buf[c]
                 total = total + dot(w, ot_buf[c], ((1,), (1,)))
             return total
 
@@ -349,30 +353,36 @@
         high, low = split(total)
         return (dot(high, table) + dot(low, table)).astype(BF)
 
-    def reduce_copies(i):
-        held_sums, taken = sums.at[i], reduce_in.at[i]
+    def first_stage(i):
         copies = []
         for a, s in enumerate(NEAR):
-            copies.append(ring_copy(a, i, s, held_sums.at[near(s - FAR)], taken.at[a], reduce_sems))
-            copies.append(ring_copy(4 + a, i, s, held_sums.at[near(s + FAR)], taken.at[4 + a], reduce_sems))
-        copies.append(ring_copy(8, i, -3, held_sums.at[near(8), 0], half_in.at[i, 0], reduce_sems))
-        copies.append(ring_copy(9, i, 3, held_sums.at[near(8), 1], half_in.at[i, 1], reduce_sems))
-        direct = [
-            ring_copy(10 + a, i, s, held_sums.at[near(s)], taken.at[8 + a], reduce_sems)
+            for h, far in ((0, -FAR), (1, FAR)):
+                source, target = sums.at[i, near(s + far)], reduce_in.at[i, 4 * h + a]
+                copies.append(ring_copy(4 * h + a, i, s, source, target, reduce_sems))
+        for h, s in ((0, -3), (1, 3)):
+            copies.append(ring_copy(8 + h, i, s, sums.at[i, near(8), h], half_in.at[i, h], reduce_sems))
+        return copies
+
+    def direct_stage(i):
+        return [
+            ring_copy(10 + a, i, s, sums.at[i, near(s)], reduce_in.at[i, 8 + a], reduce_sems)
             for a, s in enumerate(NEAR)
         ]
-        far = [
-            ring_copy(14 + h, i, s, collect_out.at[i, h], taken.at[12 + h], reduce_sems)
+
+    def far_stage(i):
+        return [
+            ring_copy(14 + h, i, s, collect_out.at[i, h], reduce_in.at[i, 12 + h], reduce_sems)
             for h, s in ((0, -FAR), (1, FAR))
         ]
-        return copies, direct, far
 
     def backward(row_grad):
         for i in range(pair):
             for q in range(parts):
-                part = part_of(q, 1)
+                part = part_of(q)
                 value = dot(weights_t[from_part(i * size * span, part), :], row_grad).astype(BF)
                 back_out[i, pl.ds(part * PART, PART)] = value.reshape(PART, span, width)
+                if i:
+                    back(wait_send, i - 1, q)
                 back(start, i, q)
             back_in[i, me] = back_out[i, me]
         for i in range(pair):
@@ -381,7 +391,7 @@
         for i in range(pair):
             for q in range(parts):
                 back(wait_recv, i, q)
-                part = part_of(q, -1)
+                part = part_of(-q)
                 got = back_in[i, pl.ds(part * PART, PART)].reshape(depth, width)
                 value = dot(placer[:, from_part(0, part)], got)
                 if q:
@@ -390,13 +400,12 @@
                     acc_buf[...] = value
                 else:
                     sums[i] = value.astype(BF).reshape(length, 2, own, width)
-            copies, direct, _ = reduce_copies(i)
-            for copy in copies + direct:
+            for copy in first_stage(i) + (direct_stage(i) if i < pair - 1 else []):
                 copy.start()
 
     def collect(i):
-        copies, _, far = reduce_copies(i)
-        for copy in copies:
+        far = far_stage(i)
+        for copy in first_stage(i):
             copy.wait_recv()
         for h, s in ((0, -FAR), (1, FAR)):
             value = sums[i, near(s)].astype(F32)
@@ -407,9 +416,8 @@
             far[h].start()
 
     def reduced(i):
-        _, direct, far = reduce_copies(i)
         grad = sums[i, z].astype(F32)
-        for copy in direct + far:
+        for copy in direct_stage(i) + far_stage(i):
             copy.wait_recv()
         for a in range(6):
             grad = grad + reduce_in[i, 8 + a].astype(F32)
@@ -425,6 +433,9 @@
         backward(interact())
         for i in range(pair):
             collect(i)
+            if i == 0:
+                for copy in direct_stage(pair - 1):
+                    copy.start()
         for i in range(pair):
             grad = reduced(i)
             total = total_buf[i] + grad
@@ -442,11 +453,10 @@
                 last_in[i, me] = last_out[i, core]
 
         for i in range(pair):
-            copies, direct, far = reduce_copies(i)
-            for copy in copies + direct + far:
+            for copy in first_stage(i) + direct_stage(i) + far_stage(i):
                 copy.wait_send()
-            for q in range(parts):
-                back(wait_send, i, q)
+        for q in range(parts):
+            back(wait_send, pair - 1, q)
         return carry
 
     lax.fori_loop(0, STEPS, one_step, 0)

time: 152 us -> 149 us (0.980)
  Pallas kernels: 147 us -> 143 us
    pallas_call x1, Pallas kernels: 147 us -> 143 us  [per_device(): pl.pallas_call(functools.partial(whole_kernel, size, length), out_shape=(...]
where the time goes in v4:
time: 149 us
  Pallas kernels  143 us (96%)
  local copies, waits for them, and re-layouts  4.48 us (3%)
    pallas_call x1, Pallas kernels, per_device(): pl.pallas_call(functools.partial(whole_kernel, size, length), out_shape=(...  143 us
    unnamed x12, local copies, waits for them, and re-layouts  3 us

profile of v4, /device:TPU:1, one launch (start us, length us, event | category | flops | bytes accessed | tf_op | source)
XLA Modules:
  0.0 148.7 jit_solution(1548971999036688460)
XLA Ops:
  0.6 0.0 copy-start.1
  0.6 0.8 reshape.10.labels_ref
  1.5 0.0 copy-start.2
  1.5 0.0 copy-start.3
  1.5 0.0 copy-start.4
  1.5 1.0 copy.10.rows_ref
  2.5 0.0 copy-done.1
  2.5 0.0 copy-done.2
  2.5 0.0 copy-done.3
  2.5 0.0 copy-done.4
  2.5 0.0 copy-start
  2.5 1.0 copy-done
  3.6 143.4 %shard_map.86 = (f32[1024,256]{1,0:T(8,128)S(1)}, f32[64,8]{1,0:T(8,128)S(1)}) custom-call(s32[2]{0:T(128)S(1)} %copy-done.4, bf16[1024,256]{1,0:T(8,128)(2,1)S(1)} %copy-done, bf16[2,64,1024]{2,1,0:T(8,128)(2,1)S(1)} %copy-done.1, s32[2,16]{1,0:T(2,128)S(1)} %copy-done.3, s32[512,32]{1,0:T(8,128)S(1)} %copy.10.rows_ref, s32[64,8]{1,0:T(8,128)S(1)} %reshape.10.labels_ref, ...), custom_call_target="tpu_custom_call" | custom-call | tf_op jit(solution)/shard_map/pallas_call | solution.py:494
  147.0 0.7 reshape.11
  147.7 1.0 copy.12
Async XLA Ops:
  0.6 1.8 %copy-start.1 = (bf16[2,64,1024]{2,1,0:T(8,128)(2,1)S(1)}, bf16[2,64,1024]{2,1,0:T(8,128)(2,1)}, u32[]{:S(2)}) copy-start(bf16[2,64,1024]{2,1,0:T(8,128)(2,1)} %coefs_ref.1) | copy-start | bytes 786436
  1.5 1.0 copy-start.2
  1.5 1.0 copy-start.3
  1.5 1.0 copy-start.4
  2.5 1.0 copy-start
